TPU v7x, 512 devices: a whole 4x4x16 slice. The times are simulated.
512 devices in a mesh: seq: 16 (over z), head: 32 (over x, y, core).
Axes of the slice: x: 4, y: 4, z: 16, core: 2. Of those that a mesh axis runs over, the one named last changes fastest.
Arguments:
- queries: bfloat16 [16384, 8192], P('seq', 'head'), may hold values from -6 to 6
- keys: bfloat16 [16384, 8192], P('seq', 'head'), may hold values from -1 to 1
- values: bfloat16 [16384, 8192], P('seq', 'head'), may hold values from -40 to 40
- log_decay: float32 [64, 16384], P('head', 'seq'), may hold values from -1 to 0
- gain: float32 [8192], P('head'), may hold values from 0.25 to 1.75
- out_grad: bfloat16 [16384, 8192], P('seq', 'head'), may hold values from -16 to 16
Outputs:
- output: bfloat16 [16384, 8192], P('seq', 'head')
- query_grad: bfloat16 [16384, 8192], P('seq', 'head')
- key_grad: bfloat16 [16384, 8192], P('seq', 'head')
- value_grad: bfloat16 [16384, 8192], P('seq', 'head')
- gain_grad: float32 [8192], P('head')
All inputs are finite; a program needn't handle non-finite values.
Results may differ from a plain program's by a relative error of at most 0.001.
Values sent between devices are 32-bit elements; how exact they have to be, the bound alone decides.
No kernel may reach another device: no remote copies, remote signals or barrier semaphores. Data moves between devices by JAX's collectives and lax.ppermute only.
A program may use at most 64 MiB of HBM per device.

v0:
```python
import jax
import jax.numpy as jnp
from jax import lax
from jax.sharding import PartitionSpec as P

epsilon = 1e-06
highest = lax.Precision.HIGHEST


def passed_along(value, axis, steps):
    count = lax.axis_size(axis)
    initial, last = (max(0, -steps), min(count, count - steps))
    return lax.ppermute(value, axis, [(source, source + steps) for source in range(initial, last)])


def to_blocks(matrix, heads_local, block_count, block_rows):
    head_width = matrix.shape[1] // heads_local
    return matrix.reshape(block_count, block_rows, heads_local, head_width).transpose(2, 0, 1, 3)


def from_blocks(blocked):
    heads_local, block_count, block_rows, head_width = blocked.shape
    return blocked.transpose(1, 2, 0, 3).reshape(block_count * block_rows, heads_local * head_width)


def carry_forward(device_decay, device_state):

    def relay_step(iteration, prefix):
        outgoing = jnp.exp(device_decay)[:, None, None] * prefix + device_state
        return passed_along(outgoing, "seq", 1)

    return lax.fori_loop(0, lax.axis_size("seq") - 1, relay_step, jnp.zeros_like(device_state))


def carry_backward(device_decay, device_back):

    def relay_step(iteration, suffix):
        outgoing = jnp.exp(device_decay)[:, None, None] * suffix + device_back
        return passed_along(outgoing, "seq", -1)

    return lax.fori_loop(0, lax.axis_size("seq") - 1, relay_step, jnp.zeros_like(device_back))


def local(queries, keys, values, log_decay, gain, out_grad):
    token_rows, channels = queries.shape
    heads_local = log_decay.shape[0]
    block_rows = min(256, token_rows)
    block_count = token_rows // block_rows
    total_channels = channels * lax.axis_size("head")
    query_narrow = to_blocks(queries, heads_local, block_count, block_rows)
    key_narrow = to_blocks(keys, heads_local, block_count, block_rows)
    query_blocks = query_narrow.astype(jnp.float32)
    key_blocks = key_narrow.astype(jnp.float32)
    value_blocks = to_blocks(values, heads_local, block_count, block_rows).astype(jnp.float32)
    decay_sum = jnp.cumsum(log_decay.reshape(heads_local, block_count, block_rows), axis=2)
    block_total = decay_sum[:, :, -1]
    causal = jnp.arange(block_rows)[:, None] >= jnp.arange(block_rows)[None, :]
    mask_decay = jnp.exp(
        jnp.where(causal, decay_sum[..., :, None] - decay_sum[..., None, :], -1e30)
    )
    from_start = jnp.exp(decay_sum)[..., None]
    to_end = jnp.exp(block_total[..., None] - decay_sum)[..., None]
    scores = (
        jnp.einsum("hnid,hnjd->hnij", query_narrow, key_narrow, preferred_element_type=jnp.float32)
        * mask_decay
    )
    inside = jnp.einsum("hnij,hnjd->hnid", scores, value_blocks, precision=highest)
    own_states = jnp.einsum("hnjd,hnje->hnde", key_blocks * to_end, value_blocks, precision=highest)
    device_decay = jnp.sum(block_total, axis=1)
    device_state = jnp.zeros_like(own_states[:, 0])
    for block_index in range(block_count):
        device_state = (
            jnp.exp(block_total[:, block_index])[:, None, None] * device_state
            + own_states[:, block_index]
        )
    incoming = carry_forward(device_decay, device_state)
    entering = []
    running = incoming
    for block_index in range(block_count):
        entering.append(running)
        running = (
            jnp.exp(block_total[:, block_index])[:, None, None] * running
            + own_states[:, block_index]
        )
    entering = jnp.stack(entering, axis=1)
    attended = inside + from_start * jnp.einsum(
        "hnid,hnde->hnie", query_blocks, entering, precision=highest
    )
    flattened = from_blocks(attended)
    grad_wide = out_grad.astype(jnp.float32)
    normed_grad = grad_wide * gain
    squares = lax.psum(jnp.sum(flattened * flattened, axis=1), "head")
    inverse = 1.0 / jnp.sqrt(squares / total_channels + epsilon)
    normed = flattened * inverse[:, None]
    projected = lax.psum(jnp.sum(normed_grad * normed, axis=1), "head")
    output = (normed * gain).astype(jnp.bfloat16)
    gain_part = jnp.sum(grad_wide * normed, axis=0)
    flat_grad = (normed_grad - normed * (projected / total_channels)[:, None]) * inverse[:, None]
    attended_grad = to_blocks(flat_grad, heads_local, block_count, block_rows)
    score_grad = (
        jnp.einsum("hnid,hnjd->hnij", attended_grad, value_blocks, precision=highest) * mask_decay
    )
    query_grad = jnp.einsum("hnij,hnjd->hnid", score_grad, key_blocks, precision=highest)
    query_grad = query_grad + from_start * jnp.einsum(
        "hnie,hnde->hnid", attended_grad, entering, precision=highest
    )
    key_grad = jnp.einsum("hnij,hnid->hnjd", score_grad, query_blocks, precision=highest)
    value_grad = jnp.einsum("hnij,hnid->hnjd", scores, attended_grad, precision=highest)
    own_back = jnp.einsum(
        "hnid,hnie->hnde", query_blocks * from_start, attended_grad, precision=highest
    )
    device_back = jnp.zeros_like(device_state)
    for block_index in reversed(range(block_count)):
        device_back = (
            own_back[:, block_index]
            + jnp.exp(block_total[:, block_index])[:, None, None] * device_back
        )
    later_sum = carry_backward(device_decay, device_back)
    leaving = []
    running = later_sum
    for block_index in reversed(range(block_count)):
        leaving.append(running)
        running = (
            own_back[:, block_index] + jnp.exp(block_total[:, block_index])[:, None, None] * running
        )
    leaving = jnp.stack(leaving[::-1], axis=1)
    key_grad = key_grad + to_end * jnp.einsum(
        "hnje,hnde->hnjd", value_blocks, leaving, precision=highest
    )
    value_grad = value_grad + to_end * jnp.einsum(
        "hnjd,hnde->hnje", key_blocks, leaving, precision=highest
    )
    gain_grad = lax.psum(gain_part, "seq")
    return (
        output,
        from_blocks(query_grad).astype(jnp.bfloat16),
        from_blocks(key_grad).astype(jnp.bfloat16),
        from_blocks(value_grad).astype(jnp.bfloat16),
        gain_grad,
    )


def solution(mesh):
    in_specs = (
        P("seq", "head"),
        P("seq", "head"),
        P("seq", "head"),
        P("head", "seq"),
        P("head"),
        P("seq", "head"),
    )
    out_specs = (P("seq", "head"), P("seq", "head"), P("seq", "head"), P("seq", "head"), P("head"))
    return jax.shard_map(local, mesh=mesh, in_specs=in_specs, out_specs=out_specs, check_vma=False)
```

profile of v0, /device:TPU:96, one launch (start us, length us, event | category | flops | bytes accessed | tf_op | source)
XLA Modules:
  0.0 471.4 jit_solution(15646903390274113141)
XLA Ops:
  1.3 2.4 reduce-window.6
  9.9 125.4 %while.24 = (s32[]{:T(128)}, f32[2,128,128]{2,1,0:T(8,128)S(1)}, f32[2,1,1]{0,2,1:T(1,128)S(1)}, f32[2,128,128]{2,1,0:T(8,128)S(1)}, s32[]{:T(128)}) while((s32[]{:T(128)}, f32[2,128,128]{2,1,0:T(8,128)S(1)}, f32[2,1,1]{0,2,1:T(1,128)S(1)}, f32[2,128,128]{2,1,0:T(8,128)S(1)}, s32[]{:T(128)}) %tuple.63), condition=%wide.region_4.5_spmd, body=%wide.region_3.4_spmd.sunk | while | flops 65538 | bytes 917613 | solution.py:32
  10.0 5.0 %collective-permute-start = (f32[2,128,128]{2,1,0:T(8,128)S(1)}, f32[2,128,128]{2,1,0:T(8,128)S(1)}, u32[]{:S(2)}, u32[]{:S(2)}) collective-permute-start(f32[2,128,128]{2,1,0:T(8,128)S(1)} %multiply_add_fusion.10), channel_id=1, source_target_pairs={{0,32},{32,64},{64,96},{96,128},{128,160},{160,192},{192,224},{224... | collective-permute-start | bytes 393224 | tf_op jit(solution)/shard_map/while/body/eval_jaxpr/ppermute | solution.py:13
  15.0 2.7 collective-permute-done
  17.8 5.6 %collective-permute-start = (f32[2,128,128]{2,1,0:T(8,128)S(1)}, f32[2,128,128]{2,1,0:T(8,128)S(1)}, u32[]{:S(2)}, u32[]{:S(2)}) collective-permute-start(f32[2,128,128]{2,1,0:T(8,128)S(1)} %multiply_add_fusion.10), channel_id=1, source_target_pairs={{0,32},{32,64},{64,96},{96,128},{128,160},{160,192},{192,224},{224... | collective-permute-start | bytes 393224 | tf_op jit(solution)/shard_map/while/body/eval_jaxpr/ppermute | solution.py:13
  23.5 2.5 collective-permute-done
  26.0 5.6 %collective-permute-start = (f32[2,128,128]{2,1,0:T(8,128)S(1)}, f32[2,128,128]{2,1,0:T(8,128)S(1)}, u32[]{:S(2)}, u32[]{:S(2)}) collective-permute-start(f32[2,128,128]{2,1,0:T(8,128)S(1)} %multiply_add_fusion.10), channel_id=1, source_target_pairs={{0,32},{32,64},{64,96},{96,128},{128,160},{160,192},{192,224},{224... | collective-permute-start | bytes 393224 | tf_op jit(solution)/shard_map/while/body/eval_jaxpr/ppermute | solution.py:13
  31.6 2.5 collective-permute-done
  34.2 5.6 %collective-permute-start = (f32[2,128,128]{2,1,0:T(8,128)S(1)}, f32[2,128,128]{2,1,0:T(8,128)S(1)}, u32[]{:S(2)}, u32[]{:S(2)}) collective-permute-start(f32[2,128,128]{2,1,0:T(8,128)S(1)} %multiply_add_fusion.10), channel_id=1, source_target_pairs={{0,32},{32,64},{64,96},{96,128},{128,160},{160,192},{192,224},{224... | collective-permute-start | bytes 393224 | tf_op jit(solution)/shard_map/while/body/eval_jaxpr/ppermute | solution.py:13
  39.8 2.5 collective-permute-done
  42.3 5.6 %collective-permute-start = (f32[2,128,128]{2,1,0:T(8,128)S(1)}, f32[2,128,128]{2,1,0:T(8,128)S(1)}, u32[]{:S(2)}, u32[]{:S(2)}) collective-permute-start(f32[2,128,128]{2,1,0:T(8,128)S(1)} %multiply_add_fusion.10), channel_id=1, source_target_pairs={{0,32},{32,64},{64,96},{96,128},{128,160},{160,192},{192,224},{224... | collective-permute-start | bytes 393224 | tf_op jit(solution)/shard_map/while/body/eval_jaxpr/ppermute | solution.py:13
  47.9 2.5 collective-permute-done
  50.5 5.6 %collective-permute-start = (f32[2,128,128]{2,1,0:T(8,128)S(1)}, f32[2,128,128]{2,1,0:T(8,128)S(1)}, u32[]{:S(2)}, u32[]{:S(2)}) collective-permute-start(f32[2,128,128]{2,1,0:T(8,128)S(1)} %multiply_add_fusion.10), channel_id=1, source_target_pairs={{0,32},{32,64},{64,96},{96,128},{128,160},{160,192},{192,224},{224... | collective-permute-start | bytes 393224 | tf_op jit(solution)/shard_map/while/body/eval_jaxpr/ppermute | solution.py:13
  56.1 3.4 collective-permute-done
  59.6 5.6 %collective-permute-start = (f32[2,128,128]{2,1,0:T(8,128)S(1)}, f32[2,128,128]{2,1,0:T(8,128)S(1)}, u32[]{:S(2)}, u32[]{:S(2)}) collective-permute-start(f32[2,128,128]{2,1,0:T(8,128)S(1)} %multiply_add_fusion.10), channel_id=1, source_target_pairs={{0,32},{32,64},{64,96},{96,128},{128,160},{160,192},{192,224},{224... | collective-permute-start | bytes 393224 | tf_op jit(solution)/shard_map/while/body/eval_jaxpr/ppermute | solution.py:13
  65.2 3.1 collective-permute-done
  68.4 5.6 %collective-permute-start = (f32[2,128,128]{2,1,0:T(8,128)S(1)}, f32[2,128,128]{2,1,0:T(8,128)S(1)}, u32[]{:S(2)}, u32[]{:S(2)}) collective-permute-start(f32[2,128,128]{2,1,0:T(8,128)S(1)} %multiply_add_fusion.10), channel_id=1, source_target_pairs={{0,32},{32,64},{64,96},{96,128},{128,160},{160,192},{192,224},{224... | collective-permute-start | bytes 393224 | tf_op jit(solution)/shard_map/while/body/eval_jaxpr/ppermute | solution.py:13
  74.1 2.5 collective-permute-done
  76.6 5.6 %collective-permute-start = (f32[2,128,128]{2,1,0:T(8,128)S(1)}, f32[2,128,128]{2,1,0:T(8,128)S(1)}, u32[]{:S(2)}, u32[]{:S(2)}) collective-permute-start(f32[2,128,128]{2,1,0:T(8,128)S(1)} %multiply_add_fusion.10), channel_id=1, source_target_pairs={{0,32},{32,64},{64,96},{96,128},{128,160},{160,192},{192,224},{224... | collective-permute-start | bytes 393224 | tf_op jit(solution)/shard_map/while/body/eval_jaxpr/ppermute | solution.py:13
  82.2 2.5 collective-permute-done
  84.8 5.6 %collective-permute-start = (f32[2,128,128]{2,1,0:T(8,128)S(1)}, f32[2,128,128]{2,1,0:T(8,128)S(1)}, u32[]{:S(2)}, u32[]{:S(2)}) collective-permute-start(f32[2,128,128]{2,1,0:T(8,128)S(1)} %multiply_add_fusion.10), channel_id=1, source_target_pairs={{0,32},{32,64},{64,96},{96,128},{128,160},{160,192},{192,224},{224... | collective-permute-start | bytes 393224 | tf_op jit(solution)/shard_map/while/body/eval_jaxpr/ppermute | solution.py:13
  90.4 2.5 collective-permute-done
  92.9 5.6 %collective-permute-start = (f32[2,128,128]{2,1,0:T(8,128)S(1)}, f32[2,128,128]{2,1,0:T(8,128)S(1)}, u32[]{:S(2)}, u32[]{:S(2)}) collective-permute-start(f32[2,128,128]{2,1,0:T(8,128)S(1)} %multiply_add_fusion.10), channel_id=1, source_target_pairs={{0,32},{32,64},{64,96},{96,128},{128,160},{160,192},{192,224},{224... | collective-permute-start | bytes 393224 | tf_op jit(solution)/shard_map/while/body/eval_jaxpr/ppermute | solution.py:13
  98.5 2.5 collective-permute-done
  101.1 5.6 %collective-permute-start = (f32[2,128,128]{2,1,0:T(8,128)S(1)}, f32[2,128,128]{2,1,0:T(8,128)S(1)}, u32[]{:S(2)}, u32[]{:S(2)}) collective-permute-start(f32[2,128,128]{2,1,0:T(8,128)S(1)} %multiply_add_fusion.10), channel_id=1, source_target_pairs={{0,32},{32,64},{64,96},{96,128},{128,160},{160,192},{192,224},{224... | collective-permute-start | bytes 393224 | tf_op jit(solution)/shard_map/while/body/eval_jaxpr/ppermute | solution.py:13
  106.7 3.0 collective-permute-done
  109.8 5.6 %collective-permute-start = (f32[2,128,128]{2,1,0:T(8,128)S(1)}, f32[2,128,128]{2,1,0:T(8,128)S(1)}, u32[]{:S(2)}, u32[]{:S(2)}) collective-permute-start(f32[2,128,128]{2,1,0:T(8,128)S(1)} %multiply_add_fusion.10), channel_id=1, source_target_pairs={{0,32},{32,64},{64,96},{96,128},{128,160},{160,192},{192,224},{224... | collective-permute-start | bytes 393224 | tf_op jit(solution)/shard_map/while/body/eval_jaxpr/ppermute | solution.py:13
  115.4 3.5 collective-permute-done
  119.0 5.6 %collective-permute-start = (f32[2,128,128]{2,1,0:T(8,128)S(1)}, f32[2,128,128]{2,1,0:T(8,128)S(1)}, u32[]{:S(2)}, u32[]{:S(2)}) collective-permute-start(f32[2,128,128]{2,1,0:T(8,128)S(1)} %multiply_add_fusion.10), channel_id=1, source_target_pairs={{0,32},{32,64},{64,96},{96,128},{128,160},{160,192},{192,224},{224... | collective-permute-start | bytes 393224 | tf_op jit(solution)/shard_map/while/body/eval_jaxpr/ppermute | solution.py:13
  124.6 2.5 collective-permute-done
  127.2 5.6 %collective-permute-start = (f32[2,128,128]{2,1,0:T(8,128)S(1)}, f32[2,128,128]{2,1,0:T(8,128)S(1)}, u32[]{:S(2)}, u32[]{:S(2)}) collective-permute-start(f32[2,128,128]{2,1,0:T(8,128)S(1)} %multiply_add_fusion.10), channel_id=1, source_target_pairs={{0,32},{32,64},{64,96},{96,128},{128,160},{160,192},{192,224},{224... | collective-permute-start | bytes 393224 | tf_op jit(solution)/shard_map/while/body/eval_jaxpr/ppermute | solution.py:13
  132.8 2.5 collective-permute-done
  139.9 62.7 %psum.21 = f32[1024]{0:T(1024)S(1)} all-reduce(f32[1024]{0:T(1024)S(1)} %bitcast.231), channel_id=1, replica_groups=mesh['seq'=16,'head'=32] {'head'}, use_global_device_ids=true, to_apply=%region_6.7 | all-reduce | flops 1024 | bytes 8192 | tf_op jit(solution)/shard_map/psum | solution.py:92
  204.7 32.4 %psum.23 = f32[256]{0:T(256)} all-reduce(f32[256]{0:T(256)S(1)} %get-tuple-element.107), channel_id=1, replica_groups=mesh['seq'=16,'head'=32] {'seq'}, use_global_device_ids=true, to_apply=%region_12.13 | all-reduce | flops 256 | bytes 2048 | tf_op jit(solution)/shard_map/psum | solution.py:133
  237.2 62.7 %psum.22 = f32[1024]{0:T(1024)S(1)} all-reduce(f32[1024]{0:T(1024)S(1)} %get-tuple-element.108), channel_id=1, replica_groups=mesh['seq'=16,'head'=32] {'head'}, use_global_device_ids=true, to_apply=%region_8.9 | all-reduce | flops 1024 | bytes 8192 | tf_op jit(solution)/shard_map/psum | solution.py:95
  303.1 6.1 %convolution_bitcast_fusion.4 = f32[4,256,2,128]{3,1,0,2:T(8,128)} fusion(f32[2,4,256,256]{3,2,1,0:T(8,128)} %copy-done, f32[4,256,2,128]{3,2,1,0:T(2,128)S(1)} %reshape.129), kind=kOutput, calls=%fused_computation.11 | convolution fusion | flops 805306368 | bytes 4194304 | tf_op jit(solution)/shard_map/hnij,hnid->hnjd/dot_general | solution.py:108
  310.5 147.5 %while.25 = (s32[]{:T(128)}, f32[2,128,128]{2,1,0:T(8,128)S(1)}, f32[2,1,1]{0,2,1:T(1,128)}, f32[2,128,128]{2,1,0:T(8,128)S(1)}, s32[]{:T(128)}) while((s32[]{:T(128)}, f32[2,128,128]{2,1,0:T(8,128)S(1)}, f32[2,1,1]{0,2,1:T(1,128)}, f32[2,128,128]{2,1,0:T(8,128)S(1)}, s32[]{:T(128)}) %tuple.69), condition=%wide.region_10.11_spmd, body=%wide.region_9.10_spmd.sunk | while | flops 65538 | bytes 917613 | solution.py:41
  312.1 1.9 collective-permute-start.1
  314.1 6.6 %collective-permute-done.1 = f32[2,128,128]{2,1,0:T(8,128)S(1)} collective-permute-done((f32[2,128,128]{2,1,0:T(8,128)}, f32[2,128,128]{2,1,0:T(8,128)S(1)}, u32[]{:S(2)}, u32[]{:S(2)}) %collective-permute-start.1) | collective-permute-done | bytes 131104 | tf_op jit(solution)/shard_map/while/body/eval_jaxpr/ppermute | solution.py:13
  322.1 1.9 collective-permute-start.1
  324.0 6.4 %collective-permute-done.1 = f32[2,128,128]{2,1,0:T(8,128)S(1)} collective-permute-done((f32[2,128,128]{2,1,0:T(8,128)}, f32[2,128,128]{2,1,0:T(8,128)S(1)}, u32[]{:S(2)}, u32[]{:S(2)}) %collective-permute-start.1) | collective-permute-done | bytes 131104 | tf_op jit(solution)/shard_map/while/body/eval_jaxpr/ppermute | solution.py:13
  331.8 1.9 collective-permute-start.1
  333.7 6.4 %collective-permute-done.1 = f32[2,128,128]{2,1,0:T(8,128)S(1)} collective-permute-done((f32[2,128,128]{2,1,0:T(8,128)}, f32[2,128,128]{2,1,0:T(8,128)S(1)}, u32[]{:S(2)}, u32[]{:S(2)}) %collective-permute-start.1) | collective-permute-done | bytes 131104 | tf_op jit(solution)/shard_map/while/body/eval_jaxpr/ppermute | solution.py:13
  341.5 1.9 collective-permute-start.1
  343.4 6.4 %collective-permute-done.1 = f32[2,128,128]{2,1,0:T(8,128)S(1)} collective-permute-done((f32[2,128,128]{2,1,0:T(8,128)}, f32[2,128,128]{2,1,0:T(8,128)S(1)}, u32[]{:S(2)}, u32[]{:S(2)}) %collective-permute-start.1) | collective-permute-done | bytes 131104 | tf_op jit(solution)/shard_map/while/body/eval_jaxpr/ppermute | solution.py:13
  351.2 1.9 collective-permute-start.1
  353.1 6.4 %collective-permute-done.1 = f32[2,128,128]{2,1,0:T(8,128)S(1)} collective-permute-done((f32[2,128,128]{2,1,0:T(8,128)}, f32[2,128,128]{2,1,0:T(8,128)S(1)}, u32[]{:S(2)}, u32[]{:S(2)}) %collective-permute-start.1) | collective-permute-done | bytes 131104 | tf_op jit(solution)/shard_map/while/body/eval_jaxpr/ppermute | solution.py:13
  360.8 1.9 collective-permute-start.1
  362.8 6.4 %collective-permute-done.1 = f32[2,128,128]{2,1,0:T(8,128)S(1)} collective-permute-done((f32[2,128,128]{2,1,0:T(8,128)}, f32[2,128,128]{2,1,0:T(8,128)S(1)}, u32[]{:S(2)}, u32[]{:S(2)}) %collective-permute-start.1) | collective-permute-done | bytes 131104 | tf_op jit(solution)/shard_map/while/body/eval_jaxpr/ppermute | solution.py:13
  370.5 1.9 collective-permute-start.1
  372.4 6.9 %collective-permute-done.1 = f32[2,128,128]{2,1,0:T(8,128)S(1)} collective-permute-done((f32[2,128,128]{2,1,0:T(8,128)}, f32[2,128,128]{2,1,0:T(8,128)S(1)}, u32[]{:S(2)}, u32[]{:S(2)}) %collective-permute-start.1) | collective-permute-done | bytes 131104 | tf_op jit(solution)/shard_map/while/body/eval_jaxpr/ppermute | solution.py:13
  382.7 7.4 %collective-permute-done.1 = f32[2,128,128]{2,1,0:T(8,128)S(1)} collective-permute-done((f32[2,128,128]{2,1,0:T(8,128)}, f32[2,128,128]{2,1,0:T(8,128)S(1)}, u32[]{:S(2)}, u32[]{:S(2)}) %collective-permute-start.1) | collective-permute-done | bytes 131104 | tf_op jit(solution)/shard_map/while/body/eval_jaxpr/ppermute | solution.py:13
  393.4 6.6 %collective-permute-done.1 = f32[2,128,128]{2,1,0:T(8,128)S(1)} collective-permute-done((f32[2,128,128]{2,1,0:T(8,128)}, f32[2,128,128]{2,1,0:T(8,128)S(1)}, u32[]{:S(2)}, u32[]{:S(2)}) %collective-permute-start.1) | collective-permute-done | bytes 131104 | tf_op jit(solution)/shard_map/while/body/eval_jaxpr/ppermute | solution.py:13
  401.4 1.9 collective-permute-start.1
  403.3 6.4 %collective-permute-done.1 = f32[2,128,128]{2,1,0:T(8,128)S(1)} collective-permute-done((f32[2,128,128]{2,1,0:T(8,128)}, f32[2,128,128]{2,1,0:T(8,128)S(1)}, u32[]{:S(2)}, u32[]{:S(2)}) %collective-permute-start.1) | collective-permute-done | bytes 131104 | tf_op jit(solution)/shard_map/while/body/eval_jaxpr/ppermute | solution.py:13
  411.1 1.9 collective-permute-start.1
  413.0 6.4 %collective-permute-done.1 = f32[2,128,128]{2,1,0:T(8,128)S(1)} collective-permute-done((f32[2,128,128]{2,1,0:T(8,128)}, f32[2,128,128]{2,1,0:T(8,128)S(1)}, u32[]{:S(2)}, u32[]{:S(2)}) %collective-permute-start.1) | collective-permute-done | bytes 131104 | tf_op jit(solution)/shard_map/while/body/eval_jaxpr/ppermute | solution.py:13
  422.7 6.4 %collective-permute-done.1 = f32[2,128,128]{2,1,0:T(8,128)S(1)} collective-permute-done((f32[2,128,128]{2,1,0:T(8,128)}, f32[2,128,128]{2,1,0:T(8,128)S(1)}, u32[]{:S(2)}, u32[]{:S(2)}) %collective-permute-start.1) | collective-permute-done | bytes 131104 | tf_op jit(solution)/shard_map/while/body/eval_jaxpr/ppermute | solution.py:13
  430.5 1.9 collective-permute-start.1
  432.4 6.4 %collective-permute-done.1 = f32[2,128,128]{2,1,0:T(8,128)S(1)} collective-permute-done((f32[2,128,128]{2,1,0:T(8,128)}, f32[2,128,128]{2,1,0:T(8,128)S(1)}, u32[]{:S(2)}, u32[]{:S(2)}) %collective-permute-start.1) | collective-permute-done | bytes 131104 | tf_op jit(solution)/shard_map/while/body/eval_jaxpr/ppermute | solution.py:13
  440.1 1.9 collective-permute-start.1
  442.1 6.4 %collective-permute-done.1 = f32[2,128,128]{2,1,0:T(8,128)S(1)} collective-permute-done((f32[2,128,128]{2,1,0:T(8,128)}, f32[2,128,128]{2,1,0:T(8,128)S(1)}, u32[]{:S(2)}, u32[]{:S(2)}) %collective-permute-start.1) | collective-permute-done | bytes 131104 | tf_op jit(solution)/shard_map/while/body/eval_jaxpr/ppermute | solution.py:13
  449.8 1.9 collective-permute-start.1
  451.7 6.4 %collective-permute-done.1 = f32[2,128,128]{2,1,0:T(8,128)S(1)} collective-permute-done((f32[2,128,128]{2,1,0:T(8,128)}, f32[2,128,128]{2,1,0:T(8,128)S(1)}, u32[]{:S(2)}, u32[]{:S(2)}) %collective-permute-start.1) | collective-permute-done | bytes 131104 | tf_op jit(solution)/shard_map/while/body/eval_jaxpr/ppermute | solution.py:13
  (130 shorter events, 59.1 us)
Async XLA Ops:
  4.7 5.0 %copy-start.19 = (f32[2]{0:T(128)}, f32[2]{0:T(128)S(1)}, u32[]{:S(2)}) copy-start(f32[2]{0:T(128)S(1)} %get-tuple-element.109) | copy-start | bytes 28
  4.7 130.6 %copy-start.15 = (f32[2]{0:T(128)}, f32[2]{0:T(128)S(1)}, u32[]{:S(2)}) copy-start(f32[2]{0:T(128)S(1)} %get-tuple-element.111) | copy-start | bytes 28
  4.7 130.6 %copy-start.17 = (f32[2]{0:T(128)}, f32[2]{0:T(128)S(1)}, u32[]{:S(2)}) copy-start(f32[2]{0:T(128)S(1)} %get-tuple-element.112) | copy-start | bytes 28
  4.8 130.6 %copy-start.20 = (f32[2]{0:T(128)}, f32[2]{0:T(128)S(1)}, u32[]{:S(2)}) copy-start(f32[2]{0:T(128)S(1)} %get-tuple-element.110) | copy-start | bytes 28
  6.0 3.8 copy-start.11
  6.0 130.0 %copy-start.9 = (pred[256,256]{1,0:T(8,128)(4,1)}, pred[256,256]{1,0:T(8,128)(4,1)S(1)}, u32[]{:S(2)}) copy-start(pred[256,256]{1,0:T(8,128)(4,1)S(1)} %iota_compare_fusion) | copy-start | bytes 196612
  9.7 125.7 %copy-start.8 = (bf16[1024,256]{1,0:T(8,128)(2,1)S(1)}, bf16[1024,256]{1,0:T(8,128)(2,1)}, u32[]{:S(2)}) copy-start(bf16[1024,256]{1,0:T(8,128)(2,1)} %param.10) | copy-start | bytes 1572868
  10.0 7.8 %collective-permute-start = (f32[2,128,128]{2,1,0:T(8,128)S(1)}, f32[2,128,128]{2,1,0:T(8,128)S(1)}, u32[]{:S(2)}, u32[]{:S(2)}) collective-permute-start(f32[2,128,128]{2,1,0:T(8,128)S(1)} %multiply_add_fusion.10), channel_id=1, source_target_pairs={{0,32},{32,64},{64,96},{96,128},{128,160},{160,192},{192,224},{224... | collective-permute-start | bytes 393224 | tf_op jit(solution)/shard_map/while/body/eval_jaxpr/ppermute | solution.py:13
  17.8 8.1 %collective-permute-start = (f32[2,128,128]{2,1,0:T(8,128)S(1)}, f32[2,128,128]{2,1,0:T(8,128)S(1)}, u32[]{:S(2)}, u32[]{:S(2)}) collective-permute-start(f32[2,128,128]{2,1,0:T(8,128)S(1)} %multiply_add_fusion.10), channel_id=1, source_target_pairs={{0,32},{32,64},{64,96},{96,128},{128,160},{160,192},{192,224},{224... | collective-permute-start | bytes 393224 | tf_op jit(solution)/shard_map/while/body/eval_jaxpr/ppermute | solution.py:13
  26.0 8.1 %collective-permute-start = (f32[2,128,128]{2,1,0:T(8,128)S(1)}, f32[2,128,128]{2,1,0:T(8,128)S(1)}, u32[]{:S(2)}, u32[]{:S(2)}) collective-permute-start(f32[2,128,128]{2,1,0:T(8,128)S(1)} %multiply_add_fusion.10), channel_id=1, source_target_pairs={{0,32},{32,64},{64,96},{96,128},{128,160},{160,192},{192,224},{224... | collective-permute-start | bytes 393224 | tf_op jit(solution)/shard_map/while/body/eval_jaxpr/ppermute | solution.py:13
  34.2 8.1 %collective-permute-start = (f32[2,128,128]{2,1,0:T(8,128)S(1)}, f32[2,128,128]{2,1,0:T(8,128)S(1)}, u32[]{:S(2)}, u32[]{:S(2)}) collective-permute-start(f32[2,128,128]{2,1,0:T(8,128)S(1)} %multiply_add_fusion.10), channel_id=1, source_target_pairs={{0,32},{32,64},{64,96},{96,128},{128,160},{160,192},{192,224},{224... | collective-permute-start | bytes 393224 | tf_op jit(solution)/shard_map/while/body/eval_jaxpr/ppermute | solution.py:13
  42.3 8.1 %collective-permute-start = (f32[2,128,128]{2,1,0:T(8,128)S(1)}, f32[2,128,128]{2,1,0:T(8,128)S(1)}, u32[]{:S(2)}, u32[]{:S(2)}) collective-permute-start(f32[2,128,128]{2,1,0:T(8,128)S(1)} %multiply_add_fusion.10), channel_id=1, source_target_pairs={{0,32},{32,64},{64,96},{96,128},{128,160},{160,192},{192,224},{224... | collective-permute-start | bytes 393224 | tf_op jit(solution)/shard_map/while/body/eval_jaxpr/ppermute | solution.py:13
  50.5 9.0 %collective-permute-start = (f32[2,128,128]{2,1,0:T(8,128)S(1)}, f32[2,128,128]{2,1,0:T(8,128)S(1)}, u32[]{:S(2)}, u32[]{:S(2)}) collective-permute-start(f32[2,128,128]{2,1,0:T(8,128)S(1)} %multiply_add_fusion.10), channel_id=1, source_target_pairs={{0,32},{32,64},{64,96},{96,128},{128,160},{160,192},{192,224},{224... | collective-permute-start | bytes 393224 | tf_op jit(solution)/shard_map/while/body/eval_jaxpr/ppermute | solution.py:13
  59.6 8.7 %collective-permute-start = (f32[2,128,128]{2,1,0:T(8,128)S(1)}, f32[2,128,128]{2,1,0:T(8,128)S(1)}, u32[]{:S(2)}, u32[]{:S(2)}) collective-permute-start(f32[2,128,128]{2,1,0:T(8,128)S(1)} %multiply_add_fusion.10), channel_id=1, source_target_pairs={{0,32},{32,64},{64,96},{96,128},{128,160},{160,192},{192,224},{224... | collective-permute-start | bytes 393224 | tf_op jit(solution)/shard_map/while/body/eval_jaxpr/ppermute | solution.py:13
  68.4 8.1 %collective-permute-start = (f32[2,128,128]{2,1,0:T(8,128)S(1)}, f32[2,128,128]{2,1,0:T(8,128)S(1)}, u32[]{:S(2)}, u32[]{:S(2)}) collective-permute-start(f32[2,128,128]{2,1,0:T(8,128)S(1)} %multiply_add_fusion.10), channel_id=1, source_target_pairs={{0,32},{32,64},{64,96},{96,128},{128,160},{160,192},{192,224},{224... | collective-permute-start | bytes 393224 | tf_op jit(solution)/shard_map/while/body/eval_jaxpr/ppermute | solution.py:13
  76.6 8.1 %collective-permute-start = (f32[2,128,128]{2,1,0:T(8,128)S(1)}, f32[2,128,128]{2,1,0:T(8,128)S(1)}, u32[]{:S(2)}, u32[]{:S(2)}) collective-permute-start(f32[2,128,128]{2,1,0:T(8,128)S(1)} %multiply_add_fusion.10), channel_id=1, source_target_pairs={{0,32},{32,64},{64,96},{96,128},{128,160},{160,192},{192,224},{224... | collective-permute-start | bytes 393224 | tf_op jit(solution)/shard_map/while/body/eval_jaxpr/ppermute | solution.py:13
  84.8 8.1 %collective-permute-start = (f32[2,128,128]{2,1,0:T(8,128)S(1)}, f32[2,128,128]{2,1,0:T(8,128)S(1)}, u32[]{:S(2)}, u32[]{:S(2)}) collective-permute-start(f32[2,128,128]{2,1,0:T(8,128)S(1)} %multiply_add_fusion.10), channel_id=1, source_target_pairs={{0,32},{32,64},{64,96},{96,128},{128,160},{160,192},{192,224},{224... | collective-permute-start | bytes 393224 | tf_op jit(solution)/shard_map/while/body/eval_jaxpr/ppermute | solution.py:13
  92.9 8.1 %collective-permute-start = (f32[2,128,128]{2,1,0:T(8,128)S(1)}, f32[2,128,128]{2,1,0:T(8,128)S(1)}, u32[]{:S(2)}, u32[]{:S(2)}) collective-permute-start(f32[2,128,128]{2,1,0:T(8,128)S(1)} %multiply_add_fusion.10), channel_id=1, source_target_pairs={{0,32},{32,64},{64,96},{96,128},{128,160},{160,192},{192,224},{224... | collective-permute-start | bytes 393224 | tf_op jit(solution)/shard_map/while/body/eval_jaxpr/ppermute | solution.py:13
  101.1 8.6 %collective-permute-start = (f32[2,128,128]{2,1,0:T(8,128)S(1)}, f32[2,128,128]{2,1,0:T(8,128)S(1)}, u32[]{:S(2)}, u32[]{:S(2)}) collective-permute-start(f32[2,128,128]{2,1,0:T(8,128)S(1)} %multiply_add_fusion.10), channel_id=1, source_target_pairs={{0,32},{32,64},{64,96},{96,128},{128,160},{160,192},{192,224},{224... | collective-permute-start | bytes 393224 | tf_op jit(solution)/shard_map/while/body/eval_jaxpr/ppermute | solution.py:13
  109.8 9.2 %collective-permute-start = (f32[2,128,128]{2,1,0:T(8,128)S(1)}, f32[2,128,128]{2,1,0:T(8,128)S(1)}, u32[]{:S(2)}, u32[]{:S(2)}) collective-permute-start(f32[2,128,128]{2,1,0:T(8,128)S(1)} %multiply_add_fusion.10), channel_id=1, source_target_pairs={{0,32},{32,64},{64,96},{96,128},{128,160},{160,192},{192,224},{224... | collective-permute-start | bytes 393224 | tf_op jit(solution)/shard_map/while/body/eval_jaxpr/ppermute | solution.py:13
  119.0 8.1 %collective-permute-start = (f32[2,128,128]{2,1,0:T(8,128)S(1)}, f32[2,128,128]{2,1,0:T(8,128)S(1)}, u32[]{:S(2)}, u32[]{:S(2)}) collective-permute-start(f32[2,128,128]{2,1,0:T(8,128)S(1)} %multiply_add_fusion.10), channel_id=1, source_target_pairs={{0,32},{32,64},{64,96},{96,128},{128,160},{160,192},{192,224},{224... | collective-permute-start | bytes 393224 | tf_op jit(solution)/shard_map/while/body/eval_jaxpr/ppermute | solution.py:13
  127.2 8.1 %collective-permute-start = (f32[2,128,128]{2,1,0:T(8,128)S(1)}, f32[2,128,128]{2,1,0:T(8,128)S(1)}, u32[]{:S(2)}, u32[]{:S(2)}) collective-permute-start(f32[2,128,128]{2,1,0:T(8,128)S(1)} %multiply_add_fusion.10), channel_id=1, source_target_pairs={{0,32},{32,64},{64,96},{96,128},{128,160},{160,192},{192,224},{224... | collective-permute-start | bytes 393224 | tf_op jit(solution)/shard_map/while/body/eval_jaxpr/ppermute | solution.py:13
  135.3 1.4 copy-start.13
  135.4 2.7 copy-start.2
  135.4 2.7 copy-start.4
  135.4 2.7 copy-start.6
  136.7 3.2 copy-start
  138.2 66.0 %copy-start.1 = (bf16[1024,256]{1,0:T(8,128)(2,1)S(1)}, bf16[1024,256]{1,0:T(8,128)(2,1)}, u32[]{:S(2)}) copy-start(bf16[1024,256]{1,0:T(8,128)(2,1)} %param.15) | copy-start | bytes 1572868
  138.2 66.0 %copy-start.22 = (f32[256]{0:T(256)S(1)}, f32[256]{0:T(256)}, u32[]{:S(2)}) copy-start(f32[256]{0:T(256)} %param.14) | copy-start | bytes 3076
  303.1 6.1 %copy-start.14 = (f32[2,4,256]{2,1,0:T(4,128)S(1)}, f32[2,4,256]{2,1,0:T(4,128)}, u32[]{:S(2)}) copy-start(f32[2,4,256]{2,1,0:T(4,128)} %get-tuple-element.137) | copy-start | bytes 24580
  309.1 1.2 copy-start.16
  309.1 1.3 copy-start.18
  309.1 1.3 copy-start.21
  309.1 1.3 copy-start.23
  312.1 8.6 %collective-permute-start.1 = (f32[2,128,128]{2,1,0:T(8,128)}, f32[2,128,128]{2,1,0:T(8,128)S(1)}, u32[]{:S(2)}, u32[]{:S(2)}) collective-permute-start(f32[2,128,128]{2,1,0:T(8,128)} %multiply_add_fusion.11), channel_id=1, source_target_pairs={{32,0},{64,32},{96,64},{128,96},{160,128},{192,160},{224,192},{256... | collective-permute-start | bytes 393224 | tf_op jit(solution)/shard_map/while/body/eval_jaxpr/ppermute | solution.py:13
  322.1 8.3 %collective-permute-start.1 = (f32[2,128,128]{2,1,0:T(8,128)}, f32[2,128,128]{2,1,0:T(8,128)S(1)}, u32[]{:S(2)}, u32[]{:S(2)}) collective-permute-start(f32[2,128,128]{2,1,0:T(8,128)} %multiply_add_fusion.11), channel_id=1, source_target_pairs={{32,0},{64,32},{96,64},{128,96},{160,128},{192,160},{224,192},{256... | collective-permute-start | bytes 393224 | tf_op jit(solution)/shard_map/while/body/eval_jaxpr/ppermute | solution.py:13
  331.8 8.3 %collective-permute-start.1 = (f32[2,128,128]{2,1,0:T(8,128)}, f32[2,128,128]{2,1,0:T(8,128)S(1)}, u32[]{:S(2)}, u32[]{:S(2)}) collective-permute-start(f32[2,128,128]{2,1,0:T(8,128)} %multiply_add_fusion.11), channel_id=1, source_target_pairs={{32,0},{64,32},{96,64},{128,96},{160,128},{192,160},{224,192},{256... | collective-permute-start | bytes 393224 | tf_op jit(solution)/shard_map/while/body/eval_jaxpr/ppermute | solution.py:13
  341.5 8.3 %collective-permute-start.1 = (f32[2,128,128]{2,1,0:T(8,128)}, f32[2,128,128]{2,1,0:T(8,128)S(1)}, u32[]{:S(2)}, u32[]{:S(2)}) collective-permute-start(f32[2,128,128]{2,1,0:T(8,128)} %multiply_add_fusion.11), channel_id=1, source_target_pairs={{32,0},{64,32},{96,64},{128,96},{160,128},{192,160},{224,192},{256... | collective-permute-start | bytes 393224 | tf_op jit(solution)/shard_map/while/body/eval_jaxpr/ppermute | solution.py:13
  351.2 8.3 %collective-permute-start.1 = (f32[2,128,128]{2,1,0:T(8,128)}, f32[2,128,128]{2,1,0:T(8,128)S(1)}, u32[]{:S(2)}, u32[]{:S(2)}) collective-permute-start(f32[2,128,128]{2,1,0:T(8,128)} %multiply_add_fusion.11), channel_id=1, source_target_pairs={{32,0},{64,32},{96,64},{128,96},{160,128},{192,160},{224,192},{256... | collective-permute-start | bytes 393224 | tf_op jit(solution)/shard_map/while/body/eval_jaxpr/ppermute | solution.py:13
  360.8 8.3 %collective-permute-start.1 = (f32[2,128,128]{2,1,0:T(8,128)}, f32[2,128,128]{2,1,0:T(8,128)S(1)}, u32[]{:S(2)}, u32[]{:S(2)}) collective-permute-start(f32[2,128,128]{2,1,0:T(8,128)} %multiply_add_fusion.11), channel_id=1, source_target_pairs={{32,0},{64,32},{96,64},{128,96},{160,128},{192,160},{224,192},{256... | collective-permute-start | bytes 393224 | tf_op jit(solution)/shard_map/while/body/eval_jaxpr/ppermute | solution.py:13
  370.5 8.9 %collective-permute-start.1 = (f32[2,128,128]{2,1,0:T(8,128)}, f32[2,128,128]{2,1,0:T(8,128)S(1)}, u32[]{:S(2)}, u32[]{:S(2)}) collective-permute-start(f32[2,128,128]{2,1,0:T(8,128)} %multiply_add_fusion.11), channel_id=1, source_target_pairs={{32,0},{64,32},{96,64},{128,96},{160,128},{192,160},{224,192},{256... | collective-permute-start | bytes 393224 | tf_op jit(solution)/shard_map/while/body/eval_jaxpr/ppermute | solution.py:13
  380.8 9.3 %collective-permute-start.1 = (f32[2,128,128]{2,1,0:T(8,128)}, f32[2,128,128]{2,1,0:T(8,128)S(1)}, u32[]{:S(2)}, u32[]{:S(2)}) collective-permute-start(f32[2,128,128]{2,1,0:T(8,128)} %multiply_add_fusion.11), channel_id=1, source_target_pairs={{32,0},{64,32},{96,64},{128,96},{160,128},{192,160},{224,192},{256... | collective-permute-start | bytes 393224 | tf_op jit(solution)/shard_map/while/body/eval_jaxpr/ppermute | solution.py:13
  391.5 8.5 %collective-permute-start.1 = (f32[2,128,128]{2,1,0:T(8,128)}, f32[2,128,128]{2,1,0:T(8,128)S(1)}, u32[]{:S(2)}, u32[]{:S(2)}) collective-permute-start(f32[2,128,128]{2,1,0:T(8,128)} %multiply_add_fusion.11), channel_id=1, source_target_pairs={{32,0},{64,32},{96,64},{128,96},{160,128},{192,160},{224,192},{256... | collective-permute-start | bytes 393224 | tf_op jit(solution)/shard_map/while/body/eval_jaxpr/ppermute | solution.py:13
  401.4 8.3 %collective-permute-start.1 = (f32[2,128,128]{2,1,0:T(8,128)}, f32[2,128,128]{2,1,0:T(8,128)S(1)}, u32[]{:S(2)}, u32[]{:S(2)}) collective-permute-start(f32[2,128,128]{2,1,0:T(8,128)} %multiply_add_fusion.11), channel_id=1, source_target_pairs={{32,0},{64,32},{96,64},{128,96},{160,128},{192,160},{224,192},{256... | collective-permute-start | bytes 393224 | tf_op jit(solution)/shard_map/while/body/eval_jaxpr/ppermute | solution.py:13
  411.1 8.3 %collective-permute-start.1 = (f32[2,128,128]{2,1,0:T(8,128)}, f32[2,128,128]{2,1,0:T(8,128)S(1)}, u32[]{:S(2)}, u32[]{:S(2)}) collective-permute-start(f32[2,128,128]{2,1,0:T(8,128)} %multiply_add_fusion.11), channel_id=1, source_target_pairs={{32,0},{64,32},{96,64},{128,96},{160,128},{192,160},{224,192},{256... | collective-permute-start | bytes 393224 | tf_op jit(solution)/shard_map/while/body/eval_jaxpr/ppermute | solution.py:13
  420.8 8.3 %collective-permute-start.1 = (f32[2,128,128]{2,1,0:T(8,128)}, f32[2,128,128]{2,1,0:T(8,128)S(1)}, u32[]{:S(2)}, u32[]{:S(2)}) collective-permute-start(f32[2,128,128]{2,1,0:T(8,128)} %multiply_add_fusion.11), channel_id=1, source_target_pairs={{32,0},{64,32},{96,64},{128,96},{160,128},{192,160},{224,192},{256... | collective-permute-start | bytes 393224 | tf_op jit(solution)/shard_map/while/body/eval_jaxpr/ppermute | solution.py:13
  430.5 8.3 %collective-permute-start.1 = (f32[2,128,128]{2,1,0:T(8,128)}, f32[2,128,128]{2,1,0:T(8,128)S(1)}, u32[]{:S(2)}, u32[]{:S(2)}) collective-permute-start(f32[2,128,128]{2,1,0:T(8,128)} %multiply_add_fusion.11), channel_id=1, source_target_pairs={{32,0},{64,32},{96,64},{128,96},{160,128},{192,160},{224,192},{256... | collective-permute-start | bytes 393224 | tf_op jit(solution)/shard_map/while/body/eval_jaxpr/ppermute | solution.py:13
  440.1 8.3 %collective-permute-start.1 = (f32[2,128,128]{2,1,0:T(8,128)}, f32[2,128,128]{2,1,0:T(8,128)S(1)}, u32[]{:S(2)}, u32[]{:S(2)}) collective-permute-start(f32[2,128,128]{2,1,0:T(8,128)} %multiply_add_fusion.11), channel_id=1, source_target_pairs={{32,0},{64,32},{96,64},{128,96},{160,128},{192,160},{224,192},{256... | collective-permute-start | bytes 393224 | tf_op jit(solution)/shard_map/while/body/eval_jaxpr/ppermute | solution.py:13
  449.8 8.3 %collective-permute-start.1 = (f32[2,128,128]{2,1,0:T(8,128)}, f32[2,128,128]{2,1,0:T(8,128)S(1)}, u32[]{:S(2)}, u32[]{:S(2)}) collective-permute-start(f32[2,128,128]{2,1,0:T(8,128)} %multiply_add_fusion.11), channel_id=1, source_target_pairs={{32,0},{64,32},{96,64},{128,96},{160,128},{192,160},{224,192},{256... | collective-permute-start | bytes 393224 | tf_op jit(solution)/shard_map/while/body/eval_jaxpr/ppermute | solution.py:13
  458.8 3.3 copy-start.10
  463.5 1.9 copy-start.12
  466.1 1.4 copy-start.3
  466.1 1.4 copy-start.5
  466.1 1.4 copy-start.7
where the time goes:
time: 473 us; the launch traced here: 471 us
  blocking collectives  158 us (33%)
  waiting for transfers between devices  138 us (29%)
  starting transfers between devices  112 us (24%)
  other arithmetic  29.4 us (6%)
  matrix products  20.7 us (4%)
  local copies, waits for them, and re-layouts  11.8 us (2%)
    ppermute x30, waiting for transfers between devices, passed_along(): lax.ppermute(value, axis, [(source, source + steps) for source in range(i...  138 us
    ppermute x30, starting transfers between devices, passed_along(): lax.ppermute(value, axis, [(source, source + steps) for source in range(i...  112 us
    psum x1, blocking collectives, local(): squares = lax.psum(jnp.sum(flattened * flattened, axis=1), 'head')  62.7 us
    psum x1, blocking collectives, local(): projected = lax.psum(jnp.sum(normed_grad * normed, axis=1), 'head')  62.7 us
    psum x1, blocking collectives, local(): gain_grad = lax.psum(gain_part, 'seq')  32.4 us
    add x15, other arithmetic, relay_step(): outgoing = jnp.exp(device_decay)[:, None, None] * suffix + device_back  21.1 us
  transfers between devices with their start and end apart: 30, of which 30 were waited for; matrix products, arithmetic and copies ran while one was open for 0% of the time, Pallas kernels for 0%

commit v1 on v0

--- a/solution.py
+++ b/solution.py
@@ -130,7 +130,11 @@
     value_grad = value_grad + to_end * jnp.einsum(
         "hnjd,hnde->hnje", key_blocks, leaving, precision=highest
     )
-    gain_grad = lax.psum(gain_part, "seq")
+    gain_grad = gain_part
+    for hop in (1, 2, 4, 8):
+        gain_grad = gain_grad + lax.ppermute(
+            gain_grad, "seq", [(dev, dev ^ hop) for dev in range(16)]
+        )
     return (
         output,
         from_blocks(query_grad).astype(jnp.bfloat16),

time: 473 us -> 462 us (0.977)
  blocking collectives: 158 us -> 126 us
  starting transfers between devices: 112 us -> 133 us
  other arithmetic: 29.4 us -> 22.7 us
  waiting for transfers between devices: 138 us -> 143 us
    psum x1 -> x0, blocking collectives: 32.4 us -> none  [local(): gain_grad = lax.psum(gain_part, 'seq')]
    ppermute x0 -> x4, starting transfers between devices: none -> 19.3 us  [local(): lax.ppermute(gain_grad, 'seq', [(dev, dev ^ hop) for dev in range(16)])]
    add x15, other arithmetic: 21.1 us -> 10.6 us  [relay_step(): outgoing = jnp.exp(device_decay)[:, None, None] * suffix + device_back]
  transfers between devices with their start and end apart: 30 -> 34, of which waited for: 30 -> 31; matrix products, arithmetic and copies ran while one was open for 0% -> 8% of each run, Pallas kernels for 0% -> 0%
where the time goes in v1:
time: 462 us; the launch traced here: 460 us
  waiting for transfers between devices  143 us (31%)
  starting transfers between devices  133 us (29%)
  blocking collectives  126 us (27%)
  other arithmetic  22.7 us (5%)
  matrix products  21.2 us (5%)
  local copies, waits for them, and re-layouts  12.3 us (3%)
    ppermute x30, waiting for transfers between devices, passed_along(): lax.ppermute(value, axis, [(source, source + steps) for source in range(i...  139 us
    ppermute x30, starting transfers between devices, passed_along(): lax.ppermute(value, axis, [(source, source + steps) for source in range(i...  114 us
    psum x1, blocking collectives, local(): projected = lax.psum(jnp.sum(normed_grad * normed, axis=1), 'head')  63.7 us
    psum x1, blocking collectives, local(): squares = lax.psum(jnp.sum(flattened * flattened, axis=1), 'head')  62.7 us
    ppermute x4, starting transfers between devices, local(): lax.ppermute(gain_grad, 'seq', [(dev, dev ^ hop) for dev in range(16)])  19.3 us
    add x15, other arithmetic, relay_step(): outgoing = jnp.exp(device_decay)[:, None, None] * suffix + device_back  10.6 us
  transfers between devices with their start and end apart: 34, of which 31 were waited for; matrix products, arithmetic and copies ran while one was open for 8% of the time, Pallas kernels for 0%

profile of v1, /device:TPU:96, one launch (start us, length us, event | category | flops | bytes accessed | tf_op | source)
XLA Modules:
  0.0 460.1 jit_solution(8078839543657161149)
XLA Ops:
  1.3 2.4 reduce-window.6
  9.8 125.4 %while.24 = (s32[]{:T(128)}, f32[2,128,128]{2,1,0:T(8,128)S(1)}, f32[2,1,1]{0,2,1:T(1,128)S(1)}, f32[2,128,128]{2,1,0:T(8,128)S(1)}, s32[]{:T(128)}) while((s32[]{:T(128)}, f32[2,128,128]{2,1,0:T(8,128)S(1)}, f32[2,1,1]{0,2,1:T(1,128)S(1)}, f32[2,128,128]{2,1,0:T(8,128)S(1)}, s32[]{:T(128)}) %tuple.63), condition=%wide.region_4.5_spmd, body=%wide.region_3.4_spmd.sunk | while | flops 65538 | bytes 917613 | solution.py:32
  9.9 5.0 %collective-permute-start = (f32[2,128,128]{2,1,0:T(8,128)S(1)}, f32[2,128,128]{2,1,0:T(8,128)S(1)}, u32[]{:S(2)}, u32[]{:S(2)}) collective-permute-start(f32[2,128,128]{2,1,0:T(8,128)S(1)} %multiply_add_fusion.10), channel_id=1, source_target_pairs={{0,32},{32,64},{64,96},{96,128},{128,160},{160,192},{192,224},{224... | collective-permute-start | bytes 393224 | tf_op jit(solution)/shard_map/while/body/eval_jaxpr/ppermute | solution.py:13
  14.9 2.7 collective-permute-done
  17.8 5.6 %collective-permute-start = (f32[2,128,128]{2,1,0:T(8,128)S(1)}, f32[2,128,128]{2,1,0:T(8,128)S(1)}, u32[]{:S(2)}, u32[]{:S(2)}) collective-permute-start(f32[2,128,128]{2,1,0:T(8,128)S(1)} %multiply_add_fusion.10), channel_id=1, source_target_pairs={{0,32},{32,64},{64,96},{96,128},{128,160},{160,192},{192,224},{224... | collective-permute-start | bytes 393224 | tf_op jit(solution)/shard_map/while/body/eval_jaxpr/ppermute | solution.py:13
  23.4 2.5 collective-permute-done
  25.9 5.6 %collective-permute-start = (f32[2,128,128]{2,1,0:T(8,128)S(1)}, f32[2,128,128]{2,1,0:T(8,128)S(1)}, u32[]{:S(2)}, u32[]{:S(2)}) collective-permute-start(f32[2,128,128]{2,1,0:T(8,128)S(1)} %multiply_add_fusion.10), channel_id=1, source_target_pairs={{0,32},{32,64},{64,96},{96,128},{128,160},{160,192},{192,224},{224... | collective-permute-start | bytes 393224 | tf_op jit(solution)/shard_map/while/body/eval_jaxpr/ppermute | solution.py:13
  31.5 2.5 collective-permute-done
  34.1 5.6 %collective-permute-start = (f32[2,128,128]{2,1,0:T(8,128)S(1)}, f32[2,128,128]{2,1,0:T(8,128)S(1)}, u32[]{:S(2)}, u32[]{:S(2)}) collective-permute-start(f32[2,128,128]{2,1,0:T(8,128)S(1)} %multiply_add_fusion.10), channel_id=1, source_target_pairs={{0,32},{32,64},{64,96},{96,128},{128,160},{160,192},{192,224},{224... | collective-permute-start | bytes 393224 | tf_op jit(solution)/shard_map/while/body/eval_jaxpr/ppermute | solution.py:13
  39.7 2.5 collective-permute-done
  42.3 5.6 %collective-permute-start = (f32[2,128,128]{2,1,0:T(8,128)S(1)}, f32[2,128,128]{2,1,0:T(8,128)S(1)}, u32[]{:S(2)}, u32[]{:S(2)}) collective-permute-start(f32[2,128,128]{2,1,0:T(8,128)S(1)} %multiply_add_fusion.10), channel_id=1, source_target_pairs={{0,32},{32,64},{64,96},{96,128},{128,160},{160,192},{192,224},{224... | collective-permute-start | bytes 393224 | tf_op jit(solution)/shard_map/while/body/eval_jaxpr/ppermute | solution.py:13
  47.8 2.5 collective-permute-done
  50.4 5.6 %collective-permute-start = (f32[2,128,128]{2,1,0:T(8,128)S(1)}, f32[2,128,128]{2,1,0:T(8,128)S(1)}, u32[]{:S(2)}, u32[]{:S(2)}) collective-permute-start(f32[2,128,128]{2,1,0:T(8,128)S(1)} %multiply_add_fusion.10), channel_id=1, source_target_pairs={{0,32},{32,64},{64,96},{96,128},{128,160},{160,192},{192,224},{224... | collective-permute-start | bytes 393224 | tf_op jit(solution)/shard_map/while/body/eval_jaxpr/ppermute | solution.py:13
  56.0 3.4 collective-permute-done
  59.5 5.6 %collective-permute-start = (f32[2,128,128]{2,1,0:T(8,128)S(1)}, f32[2,128,128]{2,1,0:T(8,128)S(1)}, u32[]{:S(2)}, u32[]{:S(2)}) collective-permute-start(f32[2,128,128]{2,1,0:T(8,128)S(1)} %multiply_add_fusion.10), channel_id=1, source_target_pairs={{0,32},{32,64},{64,96},{96,128},{128,160},{160,192},{192,224},{224... | collective-permute-start | bytes 393224 | tf_op jit(solution)/shard_map/while/body/eval_jaxpr/ppermute | solution.py:13
  65.1 3.1 collective-permute-done
  68.3 5.6 %collective-permute-start = (f32[2,128,128]{2,1,0:T(8,128)S(1)}, f32[2,128,128]{2,1,0:T(8,128)S(1)}, u32[]{:S(2)}, u32[]{:S(2)}) collective-permute-start(f32[2,128,128]{2,1,0:T(8,128)S(1)} %multiply_add_fusion.10), channel_id=1, source_target_pairs={{0,32},{32,64},{64,96},{96,128},{128,160},{160,192},{192,224},{224... | collective-permute-start | bytes 393224 | tf_op jit(solution)/shard_map/while/body/eval_jaxpr/ppermute | solution.py:13
  74.0 2.5 collective-permute-done
  76.5 5.6 %collective-permute-start = (f32[2,128,128]{2,1,0:T(8,128)S(1)}, f32[2,128,128]{2,1,0:T(8,128)S(1)}, u32[]{:S(2)}, u32[]{:S(2)}) collective-permute-start(f32[2,128,128]{2,1,0:T(8,128)S(1)} %multiply_add_fusion.10), channel_id=1, source_target_pairs={{0,32},{32,64},{64,96},{96,128},{128,160},{160,192},{192,224},{224... | collective-permute-start | bytes 393224 | tf_op jit(solution)/shard_map/while/body/eval_jaxpr/ppermute | solution.py:13
  82.1 2.5 collective-permute-done
  84.7 5.6 %collective-permute-start = (f32[2,128,128]{2,1,0:T(8,128)S(1)}, f32[2,128,128]{2,1,0:T(8,128)S(1)}, u32[]{:S(2)}, u32[]{:S(2)}) collective-permute-start(f32[2,128,128]{2,1,0:T(8,128)S(1)} %multiply_add_fusion.10), channel_id=1, source_target_pairs={{0,32},{32,64},{64,96},{96,128},{128,160},{160,192},{192,224},{224... | collective-permute-start | bytes 393224 | tf_op jit(solution)/shard_map/while/body/eval_jaxpr/ppermute | solution.py:13
  90.3 2.5 collective-permute-done
  92.9 5.6 %collective-permute-start = (f32[2,128,128]{2,1,0:T(8,128)S(1)}, f32[2,128,128]{2,1,0:T(8,128)S(1)}, u32[]{:S(2)}, u32[]{:S(2)}) collective-permute-start(f32[2,128,128]{2,1,0:T(8,128)S(1)} %multiply_add_fusion.10), channel_id=1, source_target_pairs={{0,32},{32,64},{64,96},{96,128},{128,160},{160,192},{192,224},{224... | collective-permute-start | bytes 393224 | tf_op jit(solution)/shard_map/while/body/eval_jaxpr/ppermute | solution.py:13
  98.4 2.5 collective-permute-done
  101.0 5.6 %collective-permute-start = (f32[2,128,128]{2,1,0:T(8,128)S(1)}, f32[2,128,128]{2,1,0:T(8,128)S(1)}, u32[]{:S(2)}, u32[]{:S(2)}) collective-permute-start(f32[2,128,128]{2,1,0:T(8,128)S(1)} %multiply_add_fusion.10), channel_id=1, source_target_pairs={{0,32},{32,64},{64,96},{96,128},{128,160},{160,192},{192,224},{224... | collective-permute-start | bytes 393224 | tf_op jit(solution)/shard_map/while/body/eval_jaxpr/ppermute | solution.py:13
  106.6 3.0 collective-permute-done
  109.7 5.6 %collective-permute-start = (f32[2,128,128]{2,1,0:T(8,128)S(1)}, f32[2,128,128]{2,1,0:T(8,128)S(1)}, u32[]{:S(2)}, u32[]{:S(2)}) collective-permute-start(f32[2,128,128]{2,1,0:T(8,128)S(1)} %multiply_add_fusion.10), channel_id=1, source_target_pairs={{0,32},{32,64},{64,96},{96,128},{128,160},{160,192},{192,224},{224... | collective-permute-start | bytes 393224 | tf_op jit(solution)/shard_map/while/body/eval_jaxpr/ppermute | solution.py:13
  115.3 3.5 collective-permute-done
  118.9 5.6 %collective-permute-start = (f32[2,128,128]{2,1,0:T(8,128)S(1)}, f32[2,128,128]{2,1,0:T(8,128)S(1)}, u32[]{:S(2)}, u32[]{:S(2)}) collective-permute-start(f32[2,128,128]{2,1,0:T(8,128)S(1)} %multiply_add_fusion.10), channel_id=1, source_target_pairs={{0,32},{32,64},{64,96},{96,128},{128,160},{160,192},{192,224},{224... | collective-permute-start | bytes 393224 | tf_op jit(solution)/shard_map/while/body/eval_jaxpr/ppermute | solution.py:13
  124.6 2.5 collective-permute-done
  127.1 5.6 %collective-permute-start = (f32[2,128,128]{2,1,0:T(8,128)S(1)}, f32[2,128,128]{2,1,0:T(8,128)S(1)}, u32[]{:S(2)}, u32[]{:S(2)}) collective-permute-start(f32[2,128,128]{2,1,0:T(8,128)S(1)} %multiply_add_fusion.10), channel_id=1, source_target_pairs={{0,32},{32,64},{64,96},{96,128},{128,160},{160,192},{192,224},{224... | collective-permute-start | bytes 393224 | tf_op jit(solution)/shard_map/while/body/eval_jaxpr/ppermute | solution.py:13
  132.7 2.5 collective-permute-done
  140.3 62.7 %psum.14 = f32[1024]{0:T(1024)S(1)} all-reduce(f32[1024]{0:T(1024)S(1)} %bitcast.231), channel_id=1, replica_groups=mesh['seq'=16,'head'=32] {'head'}, use_global_device_ids=true, to_apply=%region_6.7 | all-reduce | flops 1024 | bytes 8192 | tf_op jit(solution)/shard_map/psum | solution.py:92
  208.9 63.7 %psum.15 = f32[1024]{0:T(1024)} all-reduce(f32[1024]{0:T(1024)} %get-tuple-element.108), channel_id=1, replica_groups=mesh['seq'=16,'head'=32] {'head'}, use_global_device_ids=true, to_apply=%region_8.9 | all-reduce | flops 1024 | bytes 8192 | tf_op jit(solution)/shard_map/psum | solution.py:95
  273.3 2.2 fusion.16
  277.2 6.1 %convolution_bitcast_fusion.4 = f32[4,256,2,128]{3,1,0,2:T(8,128)} fusion(f32[2,4,256,256]{3,2,1,0:T(8,128)} %copy-done, f32[4,256,2,128]{3,2,1,0:T(2,128)S(1)} %reshape.129), kind=kOutput, calls=%fused_computation.11 | convolution fusion | flops 805306368 | bytes 4194304 | tf_op jit(solution)/shard_map/hnij,hnid->hnjd/dot_general | solution.py:108
  284.6 2.9 convolution_bitcast_fusion
  294.9 139.3 %while.25 = (s32[]{:T(128)}, f32[2,128,128]{2,1,0:T(8,128)S(1)}, f32[2,1,1]{0,2,1:T(1,128)}, f32[2,128,128]{2,1,0:T(8,128)S(1)}, s32[]{:T(128)}) while((s32[]{:T(128)}, f32[2,128,128]{2,1,0:T(8,128)S(1)}, f32[2,1,1]{0,2,1:T(1,128)}, f32[2,128,128]{2,1,0:T(8,128)S(1)}, s32[]{:T(128)}) %tuple.69), condition=%wide.region_10.11_spmd, body=%wide.region_9.10_spmd.sunk | while | flops 65538 | bytes 917613 | solution.py:41
  295.7 3.8 collective-permute-start.1
  299.5 9.5 %collective-permute-done.1 = f32[2,128,128]{2,1,0:T(8,128)S(1)} collective-permute-done((f32[2,128,128]{2,1,0:T(8,128)S(1)}, f32[2,128,128]{2,1,0:T(8,128)S(1)}, u32[]{:S(2)}, u32[]{:S(2)}) %collective-permute-start.1) | collective-permute-done | bytes 131104 | tf_op jit(solution)/shard_map/while/body/eval_jaxpr/ppermute | solution.py:13
  309.7 1.9 collective-permute-start.1
  311.6 6.1 %collective-permute-done.1 = f32[2,128,128]{2,1,0:T(8,128)S(1)} collective-permute-done((f32[2,128,128]{2,1,0:T(8,128)S(1)}, f32[2,128,128]{2,1,0:T(8,128)S(1)}, u32[]{:S(2)}, u32[]{:S(2)}) %collective-permute-start.1) | collective-permute-done | bytes 131104 | tf_op jit(solution)/shard_map/while/body/eval_jaxpr/ppermute | solution.py:13
  318.5 1.9 collective-permute-start.1
  320.4 6.1 %collective-permute-done.1 = f32[2,128,128]{2,1,0:T(8,128)S(1)} collective-permute-done((f32[2,128,128]{2,1,0:T(8,128)S(1)}, f32[2,128,128]{2,1,0:T(8,128)S(1)}, u32[]{:S(2)}, u32[]{:S(2)}) %collective-permute-start.1) | collective-permute-done | bytes 131104 | tf_op jit(solution)/shard_map/while/body/eval_jaxpr/ppermute | solution.py:13
  329.2 6.1 %collective-permute-done.1 = f32[2,128,128]{2,1,0:T(8,128)S(1)} collective-permute-done((f32[2,128,128]{2,1,0:T(8,128)S(1)}, f32[2,128,128]{2,1,0:T(8,128)S(1)}, u32[]{:S(2)}, u32[]{:S(2)}) %collective-permute-start.1) | collective-permute-done | bytes 131104 | tf_op jit(solution)/shard_map/while/body/eval_jaxpr/ppermute | solution.py:13
  336.0 1.9 collective-permute-start.1
  338.0 6.1 %collective-permute-done.1 = f32[2,128,128]{2,1,0:T(8,128)S(1)} collective-permute-done((f32[2,128,128]{2,1,0:T(8,128)S(1)}, f32[2,128,128]{2,1,0:T(8,128)S(1)}, u32[]{:S(2)}, u32[]{:S(2)}) %collective-permute-start.1) | collective-permute-done | bytes 131104 | tf_op jit(solution)/shard_map/while/body/eval_jaxpr/ppermute | solution.py:13
  346.8 6.5 %collective-permute-done.1 = f32[2,128,128]{2,1,0:T(8,128)S(1)} collective-permute-done((f32[2,128,128]{2,1,0:T(8,128)S(1)}, f32[2,128,128]{2,1,0:T(8,128)S(1)}, u32[]{:S(2)}, u32[]{:S(2)}) %collective-permute-start.1) | collective-permute-done | bytes 131104 | tf_op jit(solution)/shard_map/while/body/eval_jaxpr/ppermute | solution.py:13
  353.9 1.9 collective-permute-start.1
  355.9 7.5 %collective-permute-done.1 = f32[2,128,128]{2,1,0:T(8,128)S(1)} collective-permute-done((f32[2,128,128]{2,1,0:T(8,128)S(1)}, f32[2,128,128]{2,1,0:T(8,128)S(1)}, u32[]{:S(2)}, u32[]{:S(2)}) %collective-permute-start.1) | collective-permute-done | bytes 131104 | tf_op jit(solution)/shard_map/while/body/eval_jaxpr/ppermute | solution.py:13
  366.0 6.6 %collective-permute-done.1 = f32[2,128,128]{2,1,0:T(8,128)S(1)} collective-permute-done((f32[2,128,128]{2,1,0:T(8,128)S(1)}, f32[2,128,128]{2,1,0:T(8,128)S(1)}, u32[]{:S(2)}, u32[]{:S(2)}) %collective-permute-start.1) | collective-permute-done | bytes 131104 | tf_op jit(solution)/shard_map/while/body/eval_jaxpr/ppermute | solution.py:13
  375.2 6.1 %collective-permute-done.1 = f32[2,128,128]{2,1,0:T(8,128)S(1)} collective-permute-done((f32[2,128,128]{2,1,0:T(8,128)S(1)}, f32[2,128,128]{2,1,0:T(8,128)S(1)}, u32[]{:S(2)}, u32[]{:S(2)}) %collective-permute-start.1) | collective-permute-done | bytes 131104 | tf_op jit(solution)/shard_map/while/body/eval_jaxpr/ppermute | solution.py:13
  382.1 1.9 collective-permute-start.1
  384.0 6.1 %collective-permute-done.1 = f32[2,128,128]{2,1,0:T(8,128)S(1)} collective-permute-done((f32[2,128,128]{2,1,0:T(8,128)S(1)}, f32[2,128,128]{2,1,0:T(8,128)S(1)}, u32[]{:S(2)}, u32[]{:S(2)}) %collective-permute-start.1) | collective-permute-done | bytes 131104 | tf_op jit(solution)/shard_map/while/body/eval_jaxpr/ppermute | solution.py:13
  392.8 6.1 %collective-permute-done.1 = f32[2,128,128]{2,1,0:T(8,128)S(1)} collective-permute-done((f32[2,128,128]{2,1,0:T(8,128)S(1)}, f32[2,128,128]{2,1,0:T(8,128)S(1)}, u32[]{:S(2)}, u32[]{:S(2)}) %collective-permute-start.1) | collective-permute-done | bytes 131104 | tf_op jit(solution)/shard_map/while/body/eval_jaxpr/ppermute | solution.py:13
  401.6 6.1 %collective-permute-done.1 = f32[2,128,128]{2,1,0:T(8,128)S(1)} collective-permute-done((f32[2,128,128]{2,1,0:T(8,128)S(1)}, f32[2,128,128]{2,1,0:T(8,128)S(1)}, u32[]{:S(2)}, u32[]{:S(2)}) %collective-permute-start.1) | collective-permute-done | bytes 131104 | tf_op jit(solution)/shard_map/while/body/eval_jaxpr/ppermute | solution.py:13
  408.4 1.9 collective-permute-start.1
  410.3 6.3 %collective-permute-done.1 = f32[2,128,128]{2,1,0:T(8,128)S(1)} collective-permute-done((f32[2,128,128]{2,1,0:T(8,128)S(1)}, f32[2,128,128]{2,1,0:T(8,128)S(1)}, u32[]{:S(2)}, u32[]{:S(2)}) %collective-permute-start.1) | collective-permute-done | bytes 131104 | tf_op jit(solution)/shard_map/while/body/eval_jaxpr/ppermute | solution.py:13
  417.4 1.9 collective-permute-start.1
  419.3 6.1 %collective-permute-done.1 = f32[2,128,128]{2,1,0:T(8,128)S(1)} collective-permute-done((f32[2,128,128]{2,1,0:T(8,128)S(1)}, f32[2,128,128]{2,1,0:T(8,128)S(1)}, u32[]{:S(2)}, u32[]{:S(2)}) %collective-permute-start.1) | collective-permute-done | bytes 131104 | tf_op jit(solution)/shard_map/while/body/eval_jaxpr/ppermute | solution.py:13
  428.1 6.1 %collective-permute-done.1 = f32[2,128,128]{2,1,0:T(8,128)S(1)} collective-permute-done((f32[2,128,128]{2,1,0:T(8,128)S(1)}, f32[2,128,128]{2,1,0:T(8,128)S(1)}, u32[]{:S(2)}, u32[]{:S(2)}) %collective-permute-start.1) | collective-permute-done | bytes 131104 | tf_op jit(solution)/shard_map/while/body/eval_jaxpr/ppermute | solution.py:13
  434.4 4.7 %collective-permute-start.4 = (f32[256]{0:T(256)S(1)}, f32[256]{0:T(256)S(1)}, u32[]{:S(2)}, u32[]{:S(2)}) collective-permute-start(f32[256]{0:T(256)S(1)} %add.121), channel_id=1, source_target_pairs={{0,128},{32,160},{64,192},{96,224},{128,0},{160,32},{192,64},{224,... | collective-permute-start | bytes 3080 | tf_op jit(solution)/shard_map/ppermute | solution.py:135
  439.7 4.1 collective-permute-done.4
  443.9 10.8 %collective-permute-start.5 = (f32[256]{0:T(256)S(1)}, f32[256]{0:T(256)S(1)}, u32[]{:S(2)}, u32[]{:S(2)}) collective-permute-start(f32[256]{0:T(256)S(1)} %add.122), channel_id=1, source_target_pairs={{0,256},{32,288},{64,320},{96,352},{128,384},{160,416},{192,448},{... | collective-permute-start | bytes 3080 | tf_op jit(solution)/shard_map/ppermute | solution.py:135
  (143 shorter events, 60.0 us)
Async XLA Ops:
  4.7 4.9 %copy-start.20 = (f32[2]{0:T(128)}, f32[2]{0:T(128)S(1)}, u32[]{:S(2)}) copy-start(f32[2]{0:T(128)S(1)} %get-tuple-element.109) | copy-start | bytes 28
  4.7 130.5 %copy-start.14 = (f32[2]{0:T(128)}, f32[2]{0:T(128)S(1)}, u32[]{:S(2)}) copy-start(f32[2]{0:T(128)S(1)} %get-tuple-element.111) | copy-start | bytes 28
  4.7 130.5 %copy-start.17 = (f32[2]{0:T(128)}, f32[2]{0:T(128)S(1)}, u32[]{:S(2)}) copy-start(f32[2]{0:T(128)S(1)} %get-tuple-element.112) | copy-start | bytes 28
  4.7 130.5 %copy-start.22 = (f32[2]{0:T(128)}, f32[2]{0:T(128)S(1)}, u32[]{:S(2)}) copy-start(f32[2]{0:T(128)S(1)} %get-tuple-element.110) | copy-start | bytes 28
  5.4 131.0 %copy-start.8 = (pred[256,256]{1,0:T(8,128)(4,1)}, pred[256,256]{1,0:T(8,128)(4,1)S(1)}, u32[]{:S(2)}) copy-start(pred[256,256]{1,0:T(8,128)(4,1)S(1)} %iota_compare_fusion) | copy-start | bytes 196612
  9.6 126.2 %copy-start.7 = (bf16[1024,256]{1,0:T(8,128)(2,1)S(1)}, bf16[1024,256]{1,0:T(8,128)(2,1)}, u32[]{:S(2)}) copy-start(bf16[1024,256]{1,0:T(8,128)(2,1)} %param.10) | copy-start | bytes 1572868
  9.9 7.8 %collective-permute-start = (f32[2,128,128]{2,1,0:T(8,128)S(1)}, f32[2,128,128]{2,1,0:T(8,128)S(1)}, u32[]{:S(2)}, u32[]{:S(2)}) collective-permute-start(f32[2,128,128]{2,1,0:T(8,128)S(1)} %multiply_add_fusion.10), channel_id=1, source_target_pairs={{0,32},{32,64},{64,96},{96,128},{128,160},{160,192},{192,224},{224... | collective-permute-start | bytes 393224 | tf_op jit(solution)/shard_map/while/body/eval_jaxpr/ppermute | solution.py:13
  17.8 8.1 %collective-permute-start = (f32[2,128,128]{2,1,0:T(8,128)S(1)}, f32[2,128,128]{2,1,0:T(8,128)S(1)}, u32[]{:S(2)}, u32[]{:S(2)}) collective-permute-start(f32[2,128,128]{2,1,0:T(8,128)S(1)} %multiply_add_fusion.10), channel_id=1, source_target_pairs={{0,32},{32,64},{64,96},{96,128},{128,160},{160,192},{192,224},{224... | collective-permute-start | bytes 393224 | tf_op jit(solution)/shard_map/while/body/eval_jaxpr/ppermute | solution.py:13
  25.9 8.1 %collective-permute-start = (f32[2,128,128]{2,1,0:T(8,128)S(1)}, f32[2,128,128]{2,1,0:T(8,128)S(1)}, u32[]{:S(2)}, u32[]{:S(2)}) collective-permute-start(f32[2,128,128]{2,1,0:T(8,128)S(1)} %multiply_add_fusion.10), channel_id=1, source_target_pairs={{0,32},{32,64},{64,96},{96,128},{128,160},{160,192},{192,224},{224... | collective-permute-start | bytes 393224 | tf_op jit(solution)/shard_map/while/body/eval_jaxpr/ppermute | solution.py:13
  34.1 8.1 %collective-permute-start = (f32[2,128,128]{2,1,0:T(8,128)S(1)}, f32[2,128,128]{2,1,0:T(8,128)S(1)}, u32[]{:S(2)}, u32[]{:S(2)}) collective-permute-start(f32[2,128,128]{2,1,0:T(8,128)S(1)} %multiply_add_fusion.10), channel_id=1, source_target_pairs={{0,32},{32,64},{64,96},{96,128},{128,160},{160,192},{192,224},{224... | collective-permute-start | bytes 393224 | tf_op jit(solution)/shard_map/while/body/eval_jaxpr/ppermute | solution.py:13
  42.3 8.1 %collective-permute-start = (f32[2,128,128]{2,1,0:T(8,128)S(1)}, f32[2,128,128]{2,1,0:T(8,128)S(1)}, u32[]{:S(2)}, u32[]{:S(2)}) collective-permute-start(f32[2,128,128]{2,1,0:T(8,128)S(1)} %multiply_add_fusion.10), channel_id=1, source_target_pairs={{0,32},{32,64},{64,96},{96,128},{128,160},{160,192},{192,224},{224... | collective-permute-start | bytes 393224 | tf_op jit(solution)/shard_map/while/body/eval_jaxpr/ppermute | solution.py:13
  50.4 9.0 %collective-permute-start = (f32[2,128,128]{2,1,0:T(8,128)S(1)}, f32[2,128,128]{2,1,0:T(8,128)S(1)}, u32[]{:S(2)}, u32[]{:S(2)}) collective-permute-start(f32[2,128,128]{2,1,0:T(8,128)S(1)} %multiply_add_fusion.10), channel_id=1, source_target_pairs={{0,32},{32,64},{64,96},{96,128},{128,160},{160,192},{192,224},{224... | collective-permute-start | bytes 393224 | tf_op jit(solution)/shard_map/while/body/eval_jaxpr/ppermute | solution.py:13
  59.5 8.7 %collective-permute-start = (f32[2,128,128]{2,1,0:T(8,128)S(1)}, f32[2,128,128]{2,1,0:T(8,128)S(1)}, u32[]{:S(2)}, u32[]{:S(2)}) collective-permute-start(f32[2,128,128]{2,1,0:T(8,128)S(1)} %multiply_add_fusion.10), channel_id=1, source_target_pairs={{0,32},{32,64},{64,96},{96,128},{128,160},{160,192},{192,224},{224... | collective-permute-start | bytes 393224 | tf_op jit(solution)/shard_map/while/body/eval_jaxpr/ppermute | solution.py:13
  68.3 8.1 %collective-permute-start = (f32[2,128,128]{2,1,0:T(8,128)S(1)}, f32[2,128,128]{2,1,0:T(8,128)S(1)}, u32[]{:S(2)}, u32[]{:S(2)}) collective-permute-start(f32[2,128,128]{2,1,0:T(8,128)S(1)} %multiply_add_fusion.10), channel_id=1, source_target_pairs={{0,32},{32,64},{64,96},{96,128},{128,160},{160,192},{192,224},{224... | collective-permute-start | bytes 393224 | tf_op jit(solution)/shard_map/while/body/eval_jaxpr/ppermute | solution.py:13
  76.5 8.1 %collective-permute-start = (f32[2,128,128]{2,1,0:T(8,128)S(1)}, f32[2,128,128]{2,1,0:T(8,128)S(1)}, u32[]{:S(2)}, u32[]{:S(2)}) collective-permute-start(f32[2,128,128]{2,1,0:T(8,128)S(1)} %multiply_add_fusion.10), channel_id=1, source_target_pairs={{0,32},{32,64},{64,96},{96,128},{128,160},{160,192},{192,224},{224... | collective-permute-start | bytes 393224 | tf_op jit(solution)/shard_map/while/body/eval_jaxpr/ppermute | solution.py:13
  84.7 8.1 %collective-permute-start = (f32[2,128,128]{2,1,0:T(8,128)S(1)}, f32[2,128,128]{2,1,0:T(8,128)S(1)}, u32[]{:S(2)}, u32[]{:S(2)}) collective-permute-start(f32[2,128,128]{2,1,0:T(8,128)S(1)} %multiply_add_fusion.10), channel_id=1, source_target_pairs={{0,32},{32,64},{64,96},{96,128},{128,160},{160,192},{192,224},{224... | collective-permute-start | bytes 393224 | tf_op jit(solution)/shard_map/while/body/eval_jaxpr/ppermute | solution.py:13
  92.9 8.1 %collective-permute-start = (f32[2,128,128]{2,1,0:T(8,128)S(1)}, f32[2,128,128]{2,1,0:T(8,128)S(1)}, u32[]{:S(2)}, u32[]{:S(2)}) collective-permute-start(f32[2,128,128]{2,1,0:T(8,128)S(1)} %multiply_add_fusion.10), channel_id=1, source_target_pairs={{0,32},{32,64},{64,96},{96,128},{128,160},{160,192},{192,224},{224... | collective-permute-start | bytes 393224 | tf_op jit(solution)/shard_map/while/body/eval_jaxpr/ppermute | solution.py:13
  101.0 8.6 %collective-permute-start = (f32[2,128,128]{2,1,0:T(8,128)S(1)}, f32[2,128,128]{2,1,0:T(8,128)S(1)}, u32[]{:S(2)}, u32[]{:S(2)}) collective-permute-start(f32[2,128,128]{2,1,0:T(8,128)S(1)} %multiply_add_fusion.10), channel_id=1, source_target_pairs={{0,32},{32,64},{64,96},{96,128},{128,160},{160,192},{192,224},{224... | collective-permute-start | bytes 393224 | tf_op jit(solution)/shard_map/while/body/eval_jaxpr/ppermute | solution.py:13
  109.7 9.2 %collective-permute-start = (f32[2,128,128]{2,1,0:T(8,128)S(1)}, f32[2,128,128]{2,1,0:T(8,128)S(1)}, u32[]{:S(2)}, u32[]{:S(2)}) collective-permute-start(f32[2,128,128]{2,1,0:T(8,128)S(1)} %multiply_add_fusion.10), channel_id=1, source_target_pairs={{0,32},{32,64},{64,96},{96,128},{128,160},{160,192},{192,224},{224... | collective-permute-start | bytes 393224 | tf_op jit(solution)/shard_map/while/body/eval_jaxpr/ppermute | solution.py:13
  118.9 8.1 %collective-permute-start = (f32[2,128,128]{2,1,0:T(8,128)S(1)}, f32[2,128,128]{2,1,0:T(8,128)S(1)}, u32[]{:S(2)}, u32[]{:S(2)}) collective-permute-start(f32[2,128,128]{2,1,0:T(8,128)S(1)} %multiply_add_fusion.10), channel_id=1, source_target_pairs={{0,32},{32,64},{64,96},{96,128},{128,160},{160,192},{192,224},{224... | collective-permute-start | bytes 393224 | tf_op jit(solution)/shard_map/while/body/eval_jaxpr/ppermute | solution.py:13
  127.1 8.1 %collective-permute-start = (f32[2,128,128]{2,1,0:T(8,128)S(1)}, f32[2,128,128]{2,1,0:T(8,128)S(1)}, u32[]{:S(2)}, u32[]{:S(2)}) collective-permute-start(f32[2,128,128]{2,1,0:T(8,128)S(1)} %multiply_add_fusion.10), channel_id=1, source_target_pairs={{0,32},{32,64},{64,96},{96,128},{128,160},{160,192},{192,224},{224... | collective-permute-start | bytes 393224 | tf_op jit(solution)/shard_map/while/body/eval_jaxpr/ppermute | solution.py:13
  135.2 0.5 copy-start.12
  135.9 2.7 copy-start.5
  137.1 3.2 copy-start
  137.1 1.4 copy-start.10
  138.6 66.6 %copy-start.3 = (bf16[1024,256]{1,0:T(8,128)(2,1)S(1)}, bf16[1024,256]{1,0:T(8,128)(2,1)}, u32[]{:S(2)}) copy-start(bf16[1024,256]{1,0:T(8,128)(2,1)} %param.15) | copy-start | bytes 1572868
  207.0 85.3 %collective-permute-start.2 = (f32[256]{0:T(256)}, f32[256]{0:T(256)}, u32[]{:S(2)}, u32[]{:S(2)}) collective-permute-start(f32[256]{0:T(256)} %get-tuple-element.107), channel_id=1, source_target_pairs={{0,32},{32,0},{64,96},{96,64},{128,160},{160,128},{192,224},{224,1... | collective-permute-start | bytes 3080 | tf_op jit(solution)/shard_map/ppermute | solution.py:135
  277.2 6.1 %copy-start.9 = (pred[256,256]{1,0:T(8,128)(4,1)S(1)}, pred[256,256]{1,0:T(8,128)(4,1)}, u32[]{:S(2)}) copy-start(pred[256,256]{1,0:T(8,128)(4,1)} %copy-done.8) | copy-start | bytes 196612
  287.5 1.4 copy-start.13
  287.5 2.6 copy-start.6
  287.5 2.6 copy-start.11
  290.1 2.0 copy-start.15
  290.1 2.0 copy-start.18
  290.1 2.0 copy-start.23
  290.1 2.0 copy-start.24
  292.1 142.1 %copy-start.16 = (f32[2]{0:T(128)S(1)}, f32[2]{0:T(128)}, u32[]{:S(2)}) copy-start(f32[2]{0:T(128)} %copy-done.14) | copy-start | bytes 28
  292.1 142.1 %copy-start.19 = (f32[2]{0:T(128)S(1)}, f32[2]{0:T(128)}, u32[]{:S(2)}) copy-start(f32[2]{0:T(128)} %copy-done.17) | copy-start | bytes 28
  292.1 142.2 %copy-start.21 = (f32[2]{0:T(128)S(1)}, f32[2]{0:T(128)}, u32[]{:S(2)}) copy-start(f32[2]{0:T(128)} %copy-done.20) | copy-start | bytes 28
  292.1 147.0 %copy-start.2 = (f32[4,256,2,128]{3,1,0,2:T(8,128)S(1)}, f32[4,256,2,128]{3,1,0,2:T(8,128)}, u32[]{:S(2)}) copy-start(f32[4,256,2,128]{3,1,0,2:T(8,128)} %convolution_bitcast_fusion.4) | copy-start | bytes 3145732
  293.0 141.3 %collective-permute-start.3 = (f32[256]{0:T(256)S(1)}, f32[256]{0:T(256)S(1)}, u32[]{:S(2)}, u32[]{:S(2)}) collective-permute-start(f32[256]{0:T(256)S(1)} %add.120), channel_id=1, source_target_pairs={{0,64},{32,96},{64,0},{96,32},{128,192},{160,224},{192,128},{224,1... | collective-permute-start | bytes 3080 | tf_op jit(solution)/shard_map/ppermute | solution.py:135
  295.7 13.3 %collective-permute-start.1 = (f32[2,128,128]{2,1,0:T(8,128)S(1)}, f32[2,128,128]{2,1,0:T(8,128)S(1)}, u32[]{:S(2)}, u32[]{:S(2)}) collective-permute-start(f32[2,128,128]{2,1,0:T(8,128)S(1)} %multiply_add_fusion.11), channel_id=1, source_target_pairs={{32,0},{64,32},{96,64},{128,96},{160,128},{192,160},{224,192},{256... | collective-permute-start | bytes 393224 | tf_op jit(solution)/shard_map/while/body/eval_jaxpr/ppermute | solution.py:13
  309.7 8.1 %collective-permute-start.1 = (f32[2,128,128]{2,1,0:T(8,128)S(1)}, f32[2,128,128]{2,1,0:T(8,128)S(1)}, u32[]{:S(2)}, u32[]{:S(2)}) collective-permute-start(f32[2,128,128]{2,1,0:T(8,128)S(1)} %multiply_add_fusion.11), channel_id=1, source_target_pairs={{32,0},{64,32},{96,64},{128,96},{160,128},{192,160},{224,192},{256... | collective-permute-start | bytes 393224 | tf_op jit(solution)/shard_map/while/body/eval_jaxpr/ppermute | solution.py:13
  318.5 8.1 %collective-permute-start.1 = (f32[2,128,128]{2,1,0:T(8,128)S(1)}, f32[2,128,128]{2,1,0:T(8,128)S(1)}, u32[]{:S(2)}, u32[]{:S(2)}) collective-permute-start(f32[2,128,128]{2,1,0:T(8,128)S(1)} %multiply_add_fusion.11), channel_id=1, source_target_pairs={{32,0},{64,32},{96,64},{128,96},{160,128},{192,160},{224,192},{256... | collective-permute-start | bytes 393224 | tf_op jit(solution)/shard_map/while/body/eval_jaxpr/ppermute | solution.py:13
  327.3 8.1 %collective-permute-start.1 = (f32[2,128,128]{2,1,0:T(8,128)S(1)}, f32[2,128,128]{2,1,0:T(8,128)S(1)}, u32[]{:S(2)}, u32[]{:S(2)}) collective-permute-start(f32[2,128,128]{2,1,0:T(8,128)S(1)} %multiply_add_fusion.11), channel_id=1, source_target_pairs={{32,0},{64,32},{96,64},{128,96},{160,128},{192,160},{224,192},{256... | collective-permute-start | bytes 393224 | tf_op jit(solution)/shard_map/while/body/eval_jaxpr/ppermute | solution.py:13
  336.0 8.1 %collective-permute-start.1 = (f32[2,128,128]{2,1,0:T(8,128)S(1)}, f32[2,128,128]{2,1,0:T(8,128)S(1)}, u32[]{:S(2)}, u32[]{:S(2)}) collective-permute-start(f32[2,128,128]{2,1,0:T(8,128)S(1)} %multiply_add_fusion.11), channel_id=1, source_target_pairs={{32,0},{64,32},{96,64},{128,96},{160,128},{192,160},{224,192},{256... | collective-permute-start | bytes 393224 | tf_op jit(solution)/shard_map/while/body/eval_jaxpr/ppermute | solution.py:13
  344.8 8.4 %collective-permute-start.1 = (f32[2,128,128]{2,1,0:T(8,128)S(1)}, f32[2,128,128]{2,1,0:T(8,128)S(1)}, u32[]{:S(2)}, u32[]{:S(2)}) collective-permute-start(f32[2,128,128]{2,1,0:T(8,128)S(1)} %multiply_add_fusion.11), channel_id=1, source_target_pairs={{32,0},{64,32},{96,64},{128,96},{160,128},{192,160},{224,192},{256... | collective-permute-start | bytes 393224 | tf_op jit(solution)/shard_map/while/body/eval_jaxpr/ppermute | solution.py:13
  353.9 9.4 %collective-permute-start.1 = (f32[2,128,128]{2,1,0:T(8,128)S(1)}, f32[2,128,128]{2,1,0:T(8,128)S(1)}, u32[]{:S(2)}, u32[]{:S(2)}) collective-permute-start(f32[2,128,128]{2,1,0:T(8,128)S(1)} %multiply_add_fusion.11), channel_id=1, source_target_pairs={{32,0},{64,32},{96,64},{128,96},{160,128},{192,160},{224,192},{256... | collective-permute-start | bytes 393224 | tf_op jit(solution)/shard_map/while/body/eval_jaxpr/ppermute | solution.py:13
  364.0 8.5 %collective-permute-start.1 = (f32[2,128,128]{2,1,0:T(8,128)S(1)}, f32[2,128,128]{2,1,0:T(8,128)S(1)}, u32[]{:S(2)}, u32[]{:S(2)}) collective-permute-start(f32[2,128,128]{2,1,0:T(8,128)S(1)} %multiply_add_fusion.11), channel_id=1, source_target_pairs={{32,0},{64,32},{96,64},{128,96},{160,128},{192,160},{224,192},{256... | collective-permute-start | bytes 393224 | tf_op jit(solution)/shard_map/while/body/eval_jaxpr/ppermute | solution.py:13
  373.3 8.1 %collective-permute-start.1 = (f32[2,128,128]{2,1,0:T(8,128)S(1)}, f32[2,128,128]{2,1,0:T(8,128)S(1)}, u32[]{:S(2)}, u32[]{:S(2)}) collective-permute-start(f32[2,128,128]{2,1,0:T(8,128)S(1)} %multiply_add_fusion.11), channel_id=1, source_target_pairs={{32,0},{64,32},{96,64},{128,96},{160,128},{192,160},{224,192},{256... | collective-permute-start | bytes 393224 | tf_op jit(solution)/shard_map/while/body/eval_jaxpr/ppermute | solution.py:13
  382.1 8.1 %collective-permute-start.1 = (f32[2,128,128]{2,1,0:T(8,128)S(1)}, f32[2,128,128]{2,1,0:T(8,128)S(1)}, u32[]{:S(2)}, u32[]{:S(2)}) collective-permute-start(f32[2,128,128]{2,1,0:T(8,128)S(1)} %multiply_add_fusion.11), channel_id=1, source_target_pairs={{32,0},{64,32},{96,64},{128,96},{160,128},{192,160},{224,192},{256... | collective-permute-start | bytes 393224 | tf_op jit(solution)/shard_map/while/body/eval_jaxpr/ppermute | solution.py:13
  390.8 8.1 %collective-permute-start.1 = (f32[2,128,128]{2,1,0:T(8,128)S(1)}, f32[2,128,128]{2,1,0:T(8,128)S(1)}, u32[]{:S(2)}, u32[]{:S(2)}) collective-permute-start(f32[2,128,128]{2,1,0:T(8,128)S(1)} %multiply_add_fusion.11), channel_id=1, source_target_pairs={{32,0},{64,32},{96,64},{128,96},{160,128},{192,160},{224,192},{256... | collective-permute-start | bytes 393224 | tf_op jit(solution)/shard_map/while/body/eval_jaxpr/ppermute | solution.py:13
  399.6 8.1 %collective-permute-start.1 = (f32[2,128,128]{2,1,0:T(8,128)S(1)}, f32[2,128,128]{2,1,0:T(8,128)S(1)}, u32[]{:S(2)}, u32[]{:S(2)}) collective-permute-start(f32[2,128,128]{2,1,0:T(8,128)S(1)} %multiply_add_fusion.11), channel_id=1, source_target_pairs={{32,0},{64,32},{96,64},{128,96},{160,128},{192,160},{224,192},{256... | collective-permute-start | bytes 393224 | tf_op jit(solution)/shard_map/while/body/eval_jaxpr/ppermute | solution.py:13
  408.4 8.2 %collective-permute-start.1 = (f32[2,128,128]{2,1,0:T(8,128)S(1)}, f32[2,128,128]{2,1,0:T(8,128)S(1)}, u32[]{:S(2)}, u32[]{:S(2)}) collective-permute-start(f32[2,128,128]{2,1,0:T(8,128)S(1)} %multiply_add_fusion.11), channel_id=1, source_target_pairs={{32,0},{64,32},{96,64},{128,96},{160,128},{192,160},{224,192},{256... | collective-permute-start | bytes 393224 | tf_op jit(solution)/shard_map/while/body/eval_jaxpr/ppermute | solution.py:13
  417.4 8.1 %collective-permute-start.1 = (f32[2,128,128]{2,1,0:T(8,128)S(1)}, f32[2,128,128]{2,1,0:T(8,128)S(1)}, u32[]{:S(2)}, u32[]{:S(2)}) collective-permute-start(f32[2,128,128]{2,1,0:T(8,128)S(1)} %multiply_add_fusion.11), channel_id=1, source_target_pairs={{32,0},{64,32},{96,64},{128,96},{160,128},{192,160},{224,192},{256... | collective-permute-start | bytes 393224 | tf_op jit(solution)/shard_map/while/body/eval_jaxpr/ppermute | solution.py:13
  426.1 8.1 %collective-permute-start.1 = (f32[2,128,128]{2,1,0:T(8,128)S(1)}, f32[2,128,128]{2,1,0:T(8,128)S(1)}, u32[]{:S(2)}, u32[]{:S(2)}) collective-permute-start(f32[2,128,128]{2,1,0:T(8,128)S(1)} %multiply_add_fusion.11), channel_id=1, source_target_pairs={{32,0},{64,32},{96,64},{128,96},{160,128},{192,160},{224,192},{256... | collective-permute-start | bytes 393224 | tf_op jit(solution)/shard_map/while/body/eval_jaxpr/ppermute | solution.py:13
  434.2 20.5 %copy-start.1 = (f32[4,256,2,128]{3,1,0,2:T(8,128)S(1)}, f32[4,256,2,128]{3,1,0,2:T(8,128)}, u32[]{:S(2)}) copy-start(f32[4,256,2,128]{3,1,0,2:T(8,128)} %convolution_bitcast_fusion) | copy-start | bytes 3145732
  434.4 9.5 %collective-permute-start.4 = (f32[256]{0:T(256)S(1)}, f32[256]{0:T(256)S(1)}, u32[]{:S(2)}, u32[]{:S(2)}) collective-permute-start(f32[256]{0:T(256)S(1)} %add.121), channel_id=1, source_target_pairs={{0,128},{32,160},{64,192},{96,224},{128,0},{160,32},{192,64},{224,... | collective-permute-start | bytes 3080 | tf_op jit(solution)/shard_map/ppermute | solution.py:135
  443.9 12.9 %copy-start.4 = (bf16[4,256,2,128]{1,3,0,2:T(8,128)(2,1)S(1)}, bf16[4,256,2,128]{1,3,0,2:T(8,128)(2,1)}, u32[]{:S(2)}) copy-start(bf16[4,256,2,128]{1,3,0,2:T(8,128)(2,1)} %fusion.12) | copy-start | bytes 1572868
  443.9 15.6 %collective-permute-start.5 = (f32[256]{0:T(256)S(1)}, f32[256]{0:T(256)S(1)}, u32[]{:S(2)}, u32[]{:S(2)}) collective-permute-start(f32[256]{0:T(256)S(1)} %add.122), channel_id=1, source_target_pairs={{0,256},{32,288},{64,320},{96,352},{128,384},{160,416},{192,448},{... | collective-permute-start | bytes 3080 | tf_op jit(solution)/shard_map/ppermute | solution.py:135
